TPU v7x, 256 devices: a whole 4x4x8 slice. The times are simulated.
256 devices in a mesh: gene: 4 (over z_hi), cell: 64 (over x, y, z_lo, core).
Axes of the slice: x: 4, y: 4, z: 8 (z_hi: 4, z_lo: 2; z = z_hi * 2 + z_lo), core: 2. Of those that a mesh axis runs over, the one named last changes fastest.
Arguments:
- counts: int32 [16384, 32768], P('gene', 'cell'), may hold values from 0 to 2047, as said below
- w1: bfloat16 [16384, 512], P(('gene', 'cell')), may hold values from 0.099609375 to 2
- h1: float32 [512, 32768], P(None, 'cell'), may hold values from 0.1 to 2
- w2: float32 [512, 64], replicated, may hold values from 0.1 to 2
- h2: float32 [64, 32768], P(None, 'cell'), may hold values from 0.005 to 0.1
Outputs:
- w1_new: bfloat16 [16384, 512], P(('gene', 'cell'))
- h1_new: float32 [512, 32768], P(None, 'cell')
- w2_new: float32 [512, 64], replicated
- h2_new: float32 [64, 32768], P(None, 'cell')
Inputs may be any that keep to these rules, and one draw needn't show every extreme that they name: `counts`: counts are whole numbers; a gene's and a cell's typical depth vary, and cells later in the order run deeper.
All inputs are finite; a program needn't handle non-finite values.
Results may differ from a plain program's by a relative error of at most 0.0013.
The roundings to bfloat16 on the way count: a program that leaves them out, or rounds other values in their place, can miss the bound.
Values may be sent and summed in bfloat16 or wider, within the bound.
A program may use at most 64 MiB of HBM per device.

v0:
```python
import jax
import jax.numpy as jnp
from jax import lax
from jax.sharding import PartitionSpec as P


def layer_two(h1_new, w2, h2):
    hi = lax.Precision.HIGHEST
    ratio3 = h1_new / jnp.dot(w2, h2, precision=hi)
    h2_new = h2 * jnp.dot(w2.T, ratio3, precision=hi) / jnp.sum(w2, axis=0)[:, None]
    ratio4 = h1_new / jnp.dot(w2, h2_new, precision=hi)
    w2_part = jnp.dot(ratio4, h2_new.T, precision=hi)
    h2_part = jnp.sum(h2_new, axis=1)
    return (h2_new, w2_part, h2_part)


def on_device(counts, w1, h1, w2, h2):
    w1_block = lax.all_gather(w1, "cell", axis=0, tiled=True)
    values = counts.astype(jnp.float32)
    h1_low = h1.astype(jnp.bfloat16)
    approx = jnp.dot(w1_block, h1_low, preferred_element_type=jnp.float32)
    ratio = (values / approx).astype(jnp.bfloat16)
    partial_num = lax.dot_general(
        w1_block, ratio, (((0,), (0,)), ((), ())), preferred_element_type=jnp.float32
    )
    partial_col = jnp.sum(w1_block.astype(jnp.float32), axis=0)
    h1_num, colsum = lax.psum((partial_num, partial_col), "gene")
    h1_new = h1 * h1_num / colsum[:, None]
    h1_low2 = h1_new.astype(jnp.bfloat16)
    approx2 = jnp.dot(w1_block, h1_low2, preferred_element_type=jnp.float32)
    ratio2 = (values / approx2).astype(jnp.bfloat16)
    local_rows = jnp.sum(h1_new, axis=1)
    rowsum = lax.psum(local_rows, "cell")
    w1_num = lax.psum_scatter(
        lax.dot_general(
            ratio2, h1_low2, (((1,), (1,)), ((), ())), preferred_element_type=jnp.float32
        ),
        "cell",
        scatter_dimension=0,
        tiled=True,
    )
    w1_new = (w1.astype(jnp.float32) * w1_num / rowsum[None, :]).astype(jnp.bfloat16)
    h2_new, w2_part, h2_part = layer_two(h1_new, w2, h2)
    w2_num, h2_rows = lax.psum((w2_part, h2_part), "cell")
    w2_new = w2 * w2_num / h2_rows[None, :]
    return (w1_new, h1_new, w2_new, h2_new)


def solution(mesh):
    placed = (P("gene", "cell"), P(("gene", "cell"), None), P(None, "cell"), P(), P(None, "cell"))
    return jax.shard_map(
        on_device,
        mesh=mesh,
        in_specs=placed,
        out_specs=(P(("gene", "cell"), None), P(None, "cell"), P(), P(None, "cell")),
        check_vma=False,
    )
```

profile of v0, /device:TPU:1, one launch (start us, length us, event | category | flops | bytes accessed | tf_op | source)
XLA Modules:
  0.0 995.9 jit_solution(18031313151263550134)
XLA Ops:
  7.2 0.0 all-gather.2.cloned.1.call-start
  7.2 0.7 all-gather.2.cloned.1.call-update
  7.9 0.0 copy-start.1
  7.9 0.0 copy-start
  7.9 0.0 all-reduce.4.cloned.1.call-start
  8.0 114.6 %all-gather.2.cloned.1.call-done = bf16[4096,512]{1,0:T(8,128)(2,1)} async-done(((bf16[64,512]{1,0:T(8,128)(2,1)}), bf16[4096,512]{1,0:T(8,128)(2,1)}) %all-gather.2.cloned.1.call-update) | async-done | bytes 4194320 | tf_op jit(solution)/shard_map/all_gather | solution.py:18
  122.5 11.9 %fusion.8 = f32[512,512]{0,1:T(8,128)} fusion(bf16[4096,512]{1,0:T(8,128)(2,1)} %all-gather.2.cloned.1.call-done, s32[4096,512]{1,0:T(8,128)} %param.5, f32[512,512]{1,0:T(8,128)} %param.7), kind=kOutput, calls=%fused_computation.12 | convolution fusion | flops 4301520896 | bytes 14680064 | tf_op jit(solution)/shard_map/dot_general | solution.py:23
  134.5 0.0 copy-start.5
  134.5 0.0 all-reduce.4.cloned.1.call-update
  134.5 0.0 all-reduce.6.cloned.1.call-start
  134.5 0.0 copy-done.1
  134.6 0.3 copy.9
  134.9 0.0 copy-done
  134.9 0.1 reduce_sum.38
  135.0 2.8 convert_reduce_fusion
  137.8 10.0 %psum.36 = f32[512]{0:T(512)S(1)} all-reduce(f32[512]{0:T(512)S(1)} %convert_reduce_fusion), channel_id=1, replica_groups=mesh['gene'=4,'cell'=64] {'gene'}, use_global_device_ids=true, to_apply=%region_2.0 | all-reduce | flops 512 | bytes 4096 | tf_op jit(solution)/shard_map/psum | solution.py:27
  147.8 52.4 %all-reduce.4.cloned.1.call-done = f32[512,512]{0,1:T(8,128)} async-done(((f32[512,512]{0,1:T(8,128)}), f32[512,512]{0,1:T(8,128)}) %all-reduce.4.cloned.1.call-update) | async-done | bytes 1048592 | tf_op jit(solution)/shard_map/psum | solution.py:27
  200.2 0.0 copy-done.5
  200.2 0.0 copy-start.2
  200.2 2.5 fusion.6
  202.7 1.2 fusion.16
  203.9 0.0 copy-start.3
  204.0 0.0 copy-done.2
  204.0 1.2 fusion.7
  205.1 1.5 fusion.17
  206.6 0.0 all-reduce.6.cloned.1.call-update
  206.6 0.2 reduce-scatter.2.cloned.1.call-start
  206.9 0.3 fusion.15
  207.1 0.0 copy-done.3
  207.2 12.5 %fusion.4 = f32[4096,512]{1,0:T(8,128)} fusion(s32[4096,512]{1,0:T(8,128)} %param.5, bf16[4096,512]{1,0:T(8,128)(2,1)} %all-gather.2.cloned.1.call-done, f32[512,512]{0,1:T(8,128)S(1)} %get-tuple-element.11), kind=kOutput, calls=%fused_computation.6 | convolution fusion | flops 4301783040 | bytes 22020096 | tf_op jit(solution)/shard_map/dot_general | solution.py:35
  219.6 0.0 copy-start.4
  219.6 0.0 reduce-scatter.2.cloned.1.call-update
  219.6 1.3 copy.10
  221.0 138.2 %all-reduce = (f32[512]{0:T(512)S(1)}, f32[64]{0:T(128)S(1)}) all-reduce(f32[512]{0:T(512)S(1)} %get-tuple-element.10, f32[64]{0:T(128)S(1)} %get-tuple-element.12), channel_id=1, replica_groups=mesh['gene'=4,'cell'=64] {'cell'}, use_global_device_ids=true, to_apply=%region_5.0 | all-reduce | flops 576 | bytes 4608 | tf_op jit(solution)/shard_map/psum | solution.py:33
  359.2 331.3 %all-reduce.6.cloned.1.call-done = f32[512,64]{0,1:T(8,128)} async-done(((f32[512,64]{0,1:T(8,128)}), f32[512,64]{0,1:T(8,128)}) %all-reduce.6.cloned.1.call-update) | async-done | bytes 131088 | tf_op jit(solution)/shard_map/psum | solution.py:44
  690.5 1.6 multiply_divide_fusion
  692.1 295.7 %reduce-scatter.2.cloned.1.call-done = f32[64,512]{1,0:T(8,128)} async-done(((f32[4096,512]{1,0:T(8,128)}), f32[64,512]{1,0:T(8,128)}) %reduce-scatter.2.cloned.1.call-update) | async-done | bytes 131088 | tf_op jit(solution)/shard_map/reduce_scatter | solution.py:34
  987.8 0.0 copy-done.4
  987.8 1.6 divide_convert_fusion.4
Async XLA Ops:
  7.2 115.4 %all-gather.2.cloned.1.call-start = ((), (), s32[]{:S(2)}) async-start(), calls=%async_computation.1 | async-start | bytes 4259840 | tf_op jit(solution)/shard_map/all_gather | solution.py:18
  7.9 126.6 %copy-start.1 = (f32[512,512]{1,0:T(8,128)S(1)}, f32[512,512]{1,0:T(8,128)}, u32[]{:S(2)}) copy-start(f32[512,512]{1,0:T(8,128)} %param.7) | copy-start | bytes 3145732
  7.9 127.0 %copy-start = (f32[512,64]{0,1:T(8,128)S(1)}, f32[512,64]{0,1:T(8,128)}, u32[]{:S(2)}) copy-start(f32[512,64]{0,1:T(8,128)} %param.8) | copy-start | bytes 393220
  7.9 192.3 %all-reduce.4.cloned.1.call-start = ((), (), s32[]{:S(2)}) async-start(), calls=%async_computation.2 | async-start | bytes 2097152 | tf_op jit(solution)/shard_map/psum | solution.py:27
  134.5 65.8 %copy-start.5 = (f32[64,512]{1,0:T(8,128)S(1)}, f32[64,512]{1,0:T(8,128)}, u32[]{:S(2)}) copy-start(f32[64,512]{1,0:T(8,128)} %param.9) | copy-start | bytes 393220
  134.5 556.0 %all-reduce.6.cloned.1.call-start = ((), (), s32[]{:S(2)}) async-start(), calls=%async_computation.4 | async-start | bytes 262144 | tf_op jit(solution)/shard_map/psum | solution.py:44
  200.2 3.7 copy-start.2
  203.9 3.2 copy-start.3
  206.6 781.2 %reduce-scatter.2.cloned.1.call-start = ((), (), s32[]{:S(2)}) async-start(), calls=%async_computation.3 | async-start | bytes 8519680 | tf_op jit(solution)/shard_map/reduce_scatter | solution.py:34
  219.6 768.2 %copy-start.4 = (bf16[64,512]{1,0:T(8,128)(2,1)S(1)}, bf16[64,512]{1,0:T(8,128)(2,1)}, u32[]{:S(2)}) copy-start(bf16[64,512]{1,0:T(8,128)(2,1)} %param.6) | copy-start | bytes 196612
Sparse Core Ops, SparseCore 0:
  9.9 112.6 all-gather.1
  134.6 65.5 all-reduce.3
  206.7 483.6 all-reduce.5
  692.9 294.9 reduce-scatter.1
where the time goes:
time: 999 us; the launch traced here: 996 us
  waiting for transfers between devices  795 us (80%)
  blocking collectives  148 us (15%)
  matrix products  30.7 us (3%)
  between operations  13.8 us (1%)
    psum x1, waiting for transfers between devices, on_device(): w2_num, h2_rows = lax.psum((w2_part, h2_part), 'cell')  331 us
    reduce_scatter x1, waiting for transfers between devices, on_device(): lax.psum_scatter(lax.dot_general(ratio2, h1_low2, (((1,), (1,)), ((), ())...  296 us
    psum x1, blocking collectives, on_device(): rowsum = lax.psum(local_rows, 'cell')  138 us
    all_gather x1, waiting for transfers between devices, on_device(): w1_block = lax.all_gather(w1, 'cell', axis=0, tiled=True)  115 us
    psum x1, waiting for transfers between devices, on_device(): h1_num, colsum = lax.psum((partial_num, partial_col), 'gene')  52.4 us
  transfers between devices with their start and end apart: 4, of which 4 were waited for; matrix products, arithmetic and copies ran while one was open for 2% of the time, Pallas kernels for 0%

commit v1 on v0

v1 whole, which is shorter than its diff:
```python
import functools

import jax
import jax.numpy as jnp
from jax import lax
from jax.experimental import pallas as pl
from jax.experimental.pallas import tpu as pltpu
from jax.sharding import PartitionSpec as P

NX, NY, NZ, NC = 4, 4, 2, 2
NG = 4
F32, BF16 = jnp.float32, jnp.bfloat16
HI = lax.Precision.HIGHEST

S_Z = 0
S_A2 = 1
S_A3 = S_A2 + 6
S_F = S_A3 + 6
S_CS = S_F + 8
S_N = S_CS + 3
S_HB = S_N + 3
S_E1 = S_HB + 6
S_X1 = S_E1 + 8
S_X2 = S_X1 + 6
S_ZZ = S_X2 + 6
S_SC = S_ZZ + 1
S_SZ = S_SC + 1
S_SX = S_SZ + 1
S_SY = S_SX + 3
S_SG = S_SY + 3
S_ALL = S_SG + 3


def nt(a, b, precision=None):
    return lax.dot_general(
        a, b, (((1,), (1,)), ((), ())), preferred_element_type=F32, precision=precision
    )


def kernel(
    counts,
    w1,
    h1,
    w2,
    h2,
    w1_out,
    h1_out,
    w2_out,
    h2_out,
    wg,
    cnt,
    hl,
    num,
    nrecv,
    cs,
    csr,
    hbuf,
    e1s,
    e1r,
    part,
    xr,
    xr2,
    fin,
    zr,
    sm,
    smc,
    smz,
    smx,
    smy,
    smg,
    snd,
    rcv,
    csem,
):
    g = lax.axis_index("gene")
    ci = lax.axis_index("cell")
    mx, my, mz, mc = ci // 16, (ci // 4) % 4, (ci // 2) % 2, ci % 2
    oz, oc = 1 - mz, 1 - mc

    def cell(x, y, z, c):
        return ((x * NY + y) * NZ + z) * NC + c

    def at_x(d):
        return (mx + d) % NX

    def at_y(d):
        return (my + d) % NY

    def at_g(d):
        return (g + d) % NG

    def copy(src, dst, sem, gene, to):
        return pltpu.make_async_remote_copy(
            src_ref=src,
            dst_ref=dst,
            send_sem=snd.at[sem],
            recv_sem=rcv.at[sem],
            device_id=(gene, to),
            device_id_type=pl.DeviceIdType.MESH,
        )

    sibling = cell(mx, my, mz, oc)
    z_pair = cell(mx, my, oz, mc)
    x_cell = lambda d: cell(at_x(d), my, mz, mc)
    y_cell = lambda d: cell(mx, at_y(d), mz, mc)

    read_counts = pltpu.make_async_copy(counts, cnt, csem.at[0])
    read_counts.start()

    barrier = pltpu.get_barrier_semaphore()
    partners = [(g, sibling), (g, z_pair)]
    for d in range(1, 4):
        partners += [(g, x_cell(d)), (g, y_cell(d)), (at_g(d), ci)]
    for gene, to in partners:
        pl.semaphore_signal(
            barrier, inc=1, device_id=(gene, to), device_id_type=pl.DeviceIdType.MESH
        )

    wg[mx, my, mz, mc] = w1[...]
    hl[...] = h1[...].astype(BF16)
    num[...] = jnp.zeros_like(num)
    cs[...] = jnp.zeros_like(cs)
    pl.semaphore_wait(barrier, len(partners))

    own = wg.at[mx, my, mz, mc]
    go_z = copy(own, own, S_Z, g, z_pair)
    go_z.start()
    go_z.wait_recv()

    def stage_two(h, d):
        src = wg.at[mx, my, :, mc, h]
        return copy(src, src, S_A2 + 3 * h + d - 1, g, x_cell(d) if h == 0 else y_cell(d))

    for d in (1, 3, 2):
        for h in range(2):
            stage_two(h, d).start()
    for d in (1, 3, 2):
        for h in range(2):
            stage_two(h, d).wait_recv()

    def column(h, d):
        return wg.at[:, at_y(4 - d), :, mc, 0] if h == 0 else wg.at[at_x(4 - d), :, :, mc, 1]

    def stage_three(h, d):
        src = column(h, 0)
        return copy(src, src, S_A3 + 3 * h + d - 1, g, y_cell(d) if h == 0 else x_cell(d))

    def forward(h, d):
        src = column(h, d)
        return copy(src, src, S_F + 4 * h + d, g, sibling)

    for d in (1, 3, 2):
        for h in range(2):
            stage_three(h, d).start()
    for h in range(2):
        forward(h, 0).start()

    read_counts.wait()

    def pass_on(d):
        for h in range(2):
            stage_three(h, d).wait_recv()
            forward(h, d).start()

    def first(w, v):
        approx = jnp.dot(w, hl[...], preferred_element_type=F32)
        ratio = (v.astype(F32) / approx).astype(BF16)
        add = lax.dot_general(
            w, ratio, (((0,), (0,)), ((), ())), preferred_element_type=F32
        )
        for j in range(NG):
            num[j] += add[:, j * 128 : (j + 1) * 128]
        cs[...] += jnp.sum(w.astype(F32).reshape(-1, 8, w.shape[1]), axis=0)

    def first_step(t, carry):
        d = t + t // 2 - 2 * (t // 3)
        forward(0, d).wait_recv()
        first(
            wg[:, at_y(4 - d), :, :, 0].reshape(512, 512),
            cnt[:, at_y(4 - d), :, :, 0].reshape(512, 512),
        )
        forward(1, d).wait_recv()
        first(
            wg[at_x(4 - d), :, :, :, 1].reshape(512, 512),
            cnt[at_x(4 - d), :, :, :, 1].reshape(512, 512),
        )

        @pl.when(t == 0)
        def _():
            pass_on(1)
            pass_on(3)

        @pl.when(t == 1)
        def _():
            pass_on(2)

        return carry

    lax.fori_loop(0, 4, first_step, 0)

    def send_num(d):
        return copy(num.at[at_g(d)], nrecv.at[d - 1], S_N + d - 1, at_g(d), ci)

    def send_cs(d):
        return copy(cs, csr.at[d - 1], S_CS + d - 1, at_g(d), ci)

    for d in (1, 3, 2):
        send_cs(d).start()
        send_num(d).start()
    for d in (1, 3, 2):
        send_cs(d).wait_recv()
    total = jnp.sum(cs[...] + csr[0] + csr[1] + csr[2], axis=0, keepdims=True)
    colsum = jnp.transpose(jnp.broadcast_to(total, (128, 512)))
    for d in (1, 3, 2):
        send_num(d).wait_recv()
    h1_mine = h1[:, pl.ds(pl.multiple_of(g * 128, 128), 128)]
    fresh = h1_mine * (num[g] + nrecv[0] + nrecv[1] + nrecv[2]) / colsum
    high = fresh.astype(BF16)
    hbuf[0, g] = high
    hbuf[1, g] = (fresh - high.astype(F32)).astype(BF16)

    def send_h(h, d):
        src = hbuf.at[h, g]
        return copy(src, src, S_HB + 3 * h + d - 1, at_g(d), ci)

    for h in range(2):
        for d in (1, 3, 2):
            send_h(h, d).start()
    for d in (1, 3, 2):
        send_h(0, d).wait_recv()
    for j in range(NG):
        hl[:, j * 128 : (j + 1) * 128] = hbuf[0, j]

    def second(w, v):
        approx = jnp.dot(w, hl[...], preferred_element_type=F32)
        ratio = (v.astype(F32) / approx).astype(BF16)
        return nt(ratio, hl[...]).reshape(4, 2, 32, 512)

    def pick(ref, h, i, c):
        d = i + 1
        found = ref[at_x(d), :, :, c, 0] if h == 0 else ref[:, at_y(d), :, c, 1]
        return found.reshape(256, 512)

    def to_sibling(h, i):
        return copy(e1s.at[h, i], e1r.at[h, i], S_E1 + 4 * h + i, g, sibling)

    def along(h, i):
        to = x_cell(i + 1) if h == 0 else y_cell(i + 1)
        return copy(part.at[h, i], xr.at[h, i], S_X1 + 3 * h + i, g, to)

    def second_step(i, carry):
        for h in range(2):
            e1s[h, i] = second(pick(wg, h, i, oc), pick(cnt, h, i, oc))
            to_sibling(h, i).start()
        for h in range(2):
            part[h, i] = second(pick(wg, h, i, mc), pick(cnt, h, i, mc))
        for h in range(2):
            to_sibling(h, i).wait_recv()
            part[h, i] += e1r[h, i]

            @pl.when(i < 3)
            def _():
                along(h, i).start()

        return carry

    lax.fori_loop(0, 4, second_step, 0)

    for d in (1, 3, 2):
        send_h(1, d).wait_recv()
    for j in range(NG):
        h1_out[:, j * 128 : (j + 1) * 128] = hbuf[0, j].astype(F32) + hbuf[1, j].astype(F32)
    w2_t = jnp.transpose(w2[...])
    h1_new = h1_out[...]
    ratio3 = h1_new / jnp.dot(w2[...], h2[...], precision=HI, preferred_element_type=F32)
    lift = jnp.dot(w2_t, ratio3, precision=HI, preferred_element_type=F32)
    h2_out[...] = h2[...] * lift / jnp.sum(w2_t, axis=1, keepdims=True)
    ratio4 = h1_new / jnp.dot(w2[...], h2_out[...], precision=HI, preferred_element_type=F32)
    h2_mine = h2_out[pl.ds(pl.multiple_of(g * 16, 16), 16), :]
    sm[0:16, 0:512] = nt(h2_mine, ratio4, HI)
    sm[0:16, 512:640] = jnp.broadcast_to(jnp.sum(h2_mine, axis=1, keepdims=True), (16, 128))
    sm[16:24, 0:512] = nt(jnp.ones((8, 512), F32), h1_new, HI)
    sm[16:24, 512:640] = jnp.zeros((8, 128), F32)

    sm_c = copy(sm, smc.at[1], S_SC, g, sibling)
    sm_z = copy(smc.at[0], smz, S_SZ, g, z_pair)
    sm_x = lambda d: copy(smx.at[mx], smx.at[mx], S_SX + d - 1, g, x_cell(d))
    sm_y = lambda d: copy(smy.at[my], smy.at[my], S_SY + d - 1, g, y_cell(d))
    sm_g = lambda d: copy(smg.at[g], smg.at[g], S_SG + d - 1, at_g(d), ci)

    def across(h, d):
        src = part.at[h, 3, at_y(d)] if h == 0 else part.at[h, 3, at_x(d)]
        to = y_cell(d) if h == 0 else x_cell(d)
        return copy(src, xr2.at[h, d - 1], S_X2 + 3 * h + d - 1, g, to)

    sm_c.start()
    for h in range(2):
        for i in (0, 2, 1):
            along(h, i).wait_recv()
        part[h, 3] += xr[h, 0] + xr[h, 1] + xr[h, 2]
        for d in (1, 3, 2):
            across(h, d).start()
    sm_c.wait_recv()
    smc[0] = sm[...] + smc[1]
    sm_z.start()
    sm_z.wait_recv()
    smx[mx] = smc[0] + smz[...]
    for d in (1, 3, 2):
        sm_x(d).start()
    for h in range(2):
        for d in (1, 3, 2):
            across(h, d).wait_recv()
    fin[:, 0] = part[0, 3, my] + xr2[0, 0] + xr2[0, 1] + xr2[0, 2]
    fin[:, 1] = part[1, 3, mx] + xr2[1, 0] + xr2[1, 1] + xr2[1, 2]
    last = copy(fin.at[oz], zr, S_ZZ, g, z_pair)
    last.start()
    for d in (1, 3, 2):
        sm_x(d).wait_recv()
    smy[my] = smx[0] + smx[1] + smx[2] + smx[3]
    for d in (1, 3, 2):
        sm_y(d).start()
    for d in (1, 3, 2):
        sm_y(d).wait_recv()
    done = smy[0] + smy[1] + smy[2] + smy[3]
    smg[g] = done[0:16]
    for d in (1, 3, 2):
        sm_g(d).start()
    last.wait_recv()
    w1_num = (fin[mz] + zr[...]).reshape(64, 512)
    rowsum = done[16:17, 0:512]
    w1_now = w1[...].astype(F32).reshape(64, 512)
    w1_out[...] = (w1_now * w1_num / rowsum).astype(BF16)
    for d in (1, 3, 2):
        sm_g(d).wait_recv()
    whole = smg[...].reshape(64, 640)
    w2_out[...] = jnp.transpose(w2_t * whole[:, 0:512] / whole[:, 512:513])

    go_z.wait_send()
    sm_c.wait_send()
    sm_z.wait_send()
    last.wait_send()
    for d in range(1, 4):
        for h in range(2):
            stage_two(h, d).wait_send()
            stage_three(h, d).wait_send()
            send_h(h, d).wait_send()
            along(h, d - 1).wait_send()
            across(h, d).wait_send()
        for sent in (send_num, send_cs, sm_x, sm_y, sm_g):
            sent(d).wait_send()
    for h in range(2):
        for d in range(4):
            forward(h, d).wait_send()
            to_sibling(h, d).wait_send()


def on_device(counts, w1, h1, w2, h2):
    vmem = pl.BlockSpec(memory_space=pltpu.VMEM)
    shape = (NX, NY, NZ, NC, 2, 32, 512)
    return pl.pallas_call(
        kernel,
        out_shape=(
            jax.ShapeDtypeStruct((64, 512), BF16),
            jax.ShapeDtypeStruct((512, 512), F32),
            jax.ShapeDtypeStruct((512, 64), F32),
            jax.ShapeDtypeStruct((64, 512), F32),
        ),
        in_specs=[pl.BlockSpec(memory_space=pl.ANY)] + [vmem] * 4,
        out_specs=(vmem,) * 4,
        scratch_shapes=[
            pltpu.VMEM(shape, BF16),
            pltpu.VMEM(shape, jnp.int32),
            pltpu.VMEM((512, 512), BF16),
            pltpu.VMEM((NG, 512, 128), F32),
            pltpu.VMEM((3, 512, 128), F32),
            pltpu.VMEM((8, 512), F32),
            pltpu.VMEM((3, 8, 512), F32),
            pltpu.VMEM((2, NG, 512, 128), BF16),
            pltpu.VMEM((2, 4, 4, 2, 32, 512), F32),
            pltpu.VMEM((2, 4, 4, 2, 32, 512), F32),
            pltpu.VMEM((2, 4, 4, 2, 32, 512), F32),
            pltpu.VMEM((2, 3, 4, 2, 32, 512), F32),
            pltpu.VMEM((2, 3, 2, 32, 512), F32),
            pltpu.VMEM((2, 2, 32, 512), F32),
            pltpu.VMEM((2, 32, 512), F32),
            pltpu.VMEM((24, 640), F32),
            pltpu.VMEM((2, 24, 640), F32),
            pltpu.VMEM((24, 640), F32),
            pltpu.VMEM((4, 24, 640), F32),
            pltpu.VMEM((4, 24, 640), F32),
            pltpu.VMEM((NG, 16, 640), F32),
            pltpu.SemaphoreType.DMA((S_ALL,)),
            pltpu.SemaphoreType.DMA((S_ALL,)),
            pltpu.SemaphoreType.DMA((1,)),
        ],
        compiler_params=pltpu.CompilerParams(
            collective_id=0, has_side_effects=True, vmem_limit_bytes=60 * 1024 * 1024
        ),
    )(counts.reshape(shape), w1.reshape(2, 32, 512), h1, w2, h2)


def solution(mesh):
    placed = (P("gene", "cell"), P(("gene", "cell"), None), P(None, "cell"), P(), P(None, "cell"))
    return jax.shard_map(
        on_device,
        mesh=mesh,
        in_specs=placed,
        out_specs=(P(("gene", "cell"), None), P(None, "cell"), P(), P(None, "cell")),
        check_vma=False,
    )
```

time: 999 us -> 148 us (0.15)
  waiting for transfers between devices: 795 us -> 0 us
  blocking collectives: 148 us -> 0 us
  Pallas kernels: 0 us -> 137 us
  matrix products: 30.7 us -> 0 us
  between operations: 13.8 us -> 0.64 us
    psum x2 -> x0, waiting for transfers between devices: 384 us -> none  [the longest x1 331 us: on_device(): w2_num, h2_rows = lax.psum((w2_part, h2_part), 'cell')]
    reduce_scatter x1 -> x0, waiting for transfers between devices: 296 us -> none  [on_device(): lax.psum_scatter(lax.dot_general(ratio2, h1_low2, (((1,), (1,)), ((), ())...]
    psum x2 -> x0, blocking collectives: 148 us -> none  [the longest x1 138 us: on_device(): rowsum = lax.psum(local_rows, 'cell')]
    pallas_call x0 -> x1, Pallas kernels: none -> 137 us  [on_device(): pl.pallas_call(kernel, out_shape=(jax.ShapeDtypeStruct((64, 512), BF16),...]
    all_gather x1 -> x0, waiting for transfers between devices: 115 us -> none  [on_device(): w1_block = lax.all_gather(w1, 'cell', axis=0, tiled=True)]
    dot_general x6 -> x0, matrix products: 30.7 us -> none  [the longest x1 12.5 us: on_device(): lax.dot_general(ratio2, h1_low2, (((1,), (1,)), ((), ())), preferred_elem...]
  transfers between devices with their start and end apart: 4 -> 0, of which waited for: 4 -> 0; matrix products, arithmetic and copies ran while one was open for 2% -> 0% of each run, Pallas kernels for 0% -> 0%
where the time goes in v1:
time: 148 us; the launch traced here: 147 us
  Pallas kernels  137 us (93%)
  local copies, waits for them, and re-layouts  8.76 us (6%)
    pallas_call x1, Pallas kernels, on_device(): pl.pallas_call(kernel, out_shape=(jax.ShapeDtypeStruct((64, 512), BF16),...  137 us
    unnamed x4, local copies, waits for them, and re-layouts  7.04 us

profile of v1, /device:TPU:1, one launch (start us, length us, event | category | flops | bytes accessed | tf_op | source)
XLA Modules:
  0.0 146.8 jit_solution(9090212282553090198)
XLA Ops:
  0.6 1.7 %copy.9.w2 = f32[512,64]{1,0:T(8,128)} copy(f32[512,64]{0,1:T(8,128)} %param.8) | data formatting | bytes 262144 | tf_op args[3]
  2.4 137.4 %shard_map.84 = (bf16[64,512]{1,0:T(8,128)(2,1)}, f32[512,512]{1,0:T(8,128)}, f32[512,64]{1,0:T(8,128)}, f32[64,512]{1,0:T(8,128)}) custom-call(s32[4,4,2,2,2,32,512]{6,5,4,3,2,1,0:T(8,128)} %bitcast.2, bf16[2,32,512]{2,1,0:T(8,128)(2,1)} %bitcast.3, f32[512,512]{1,0:T(8,128)} %h1.1, f32[512,64]{1,0:T(8,128)} %copy.9.w2, f32[64,512]{1,0:T(8,128)} %h2.1), custom_call_target="tpu_custom_call" | custom-call | tf_op jit(solution)/shard_map/pallas_call | solution.py:360
  139.8 1.7 %copy.10 = f32[512,64]{0,1:T(8,128)} copy(f32[512,64]{1,0:T(8,128)} %get-tuple-element.6) | data formatting | bytes 262144 | tf_op jit(solution)/shard_map/pallas_call | solution.py:360
  141.5 1.5 %copy.14 = bf16[64,512]{1,0:T(8,128)(2,1)} copy(bf16[64,512]{1,0:T(8,128)(2,1)} %get-tuple-element.12) | data formatting | bytes 131072
  143.0 2.3 %copy.15 = f32[512,512]{1,0:T(8,128)} copy(f32[512,512]{1,0:T(8,128)} %get-tuple-element.13) | data formatting | bytes 2097152
  145.3 1.6 %copy.16 = f32[64,512]{1,0:T(8,128)} copy(f32[64,512]{1,0:T(8,128)} %get-tuple-element.15) | data formatting | bytes 262144

commit v2 on v0

v2 whole, which is shorter than its diff:
```python
import jax
import jax.numpy as jnp
from jax import lax
from jax.experimental import pallas as pl
from jax.experimental.pallas import tpu as pltpu
from jax.sharding import PartitionSpec as P

NX, NY, NZ, NC = 4, 4, 2, 2
NG = 4
F32, BF16, I16 = jnp.float32, jnp.bfloat16, jnp.int16
HI = lax.Precision.HIGHEST
TOP = 32767.0
ORDER = (1, 3, 2)

SIZES = dict(
    z=1, a2=6, a3=6, f=8, m=3, n=3, hb=6, h2=3, e1=8, p=6, ps=6, q=6, qs=6, l=1, ls=1,
    s0=3, s1=1, s2=1, s3=3, s4=3, s5=3, s6=1,
)
PLACE, S_ALL = {}, 0
for _name, _size in SIZES.items():
    PLACE[_name] = S_ALL
    S_ALL += _size


def nt(a, b, precision=None):
    return lax.dot_general(
        a, b, (((1,), (1,)), ((), ())), preferred_element_type=F32, precision=precision
    )


def high(a, b):
    return jnp.dot(a, b, precision=HI, preferred_element_type=F32)


def coded(v, axis):
    most = jnp.maximum(jnp.max(v, axis=axis, keepdims=True), 1e-30)
    return jnp.round(v * (TOP / most)).astype(jnp.int32).astype(I16), most


def decoded(q, most):
    return q.astype(jnp.int32).astype(F32) * (most * (1.0 / TOP))


def kernel(
    counts, w1, h1, w2t, h2,
    w1_out, hbuf, w2t_out, h2b,
    wg, cnt, h1v, w2tv, h2v, hl, num, nq, nqr, nm, nmr, cs,
    e1s, e1r, part, acc, pq, pqr, ps, psr, aq, aqr, aps, apr, fin, lq, lqr, lps, lpr,
    sm, smr, sv, svr, sz, szr, sx, sy, sg,
    snd, rcv, loc,
):
    g = lax.axis_index("gene")
    ci = lax.axis_index("cell")
    mx, my, mz, mc = ci // 16, (ci // 4) % 4, (ci // 2) % 2, ci % 2
    oz, oc = 1 - mz, 1 - mc

    def cell(x, y, z, c):
        return ((x * NY + y) * NZ + z) * NC + c

    def at_x(d):
        return (mx + d) % NX

    def at_y(d):
        return (my + d) % NY

    def at_g(d):
        return (g + d) % NG

    def copy(src, dst, name, k, to):
        sem = PLACE[name] + k
        return pltpu.make_async_remote_copy(
            src_ref=src,
            dst_ref=dst,
            send_sem=snd.at[sem],
            recv_sem=rcv.at[sem],
            device_id=to,
            device_id_type=pl.DeviceIdType.MESH,
        )

    sibling = (g, cell(mx, my, mz, oc))
    z_pair = (g, cell(mx, my, oz, mc))

    def to_x(d):
        return (g, cell(at_x(d), my, mz, mc))

    def to_y(d):
        return (g, cell(mx, at_y(d), mz, mc))

    def to_g(d):
        return (at_g(d), ci)

    own = wg.at[mx, my, mz, mc]
    barrier = pltpu.get_barrier_semaphore()
    partners = [sibling, z_pair]
    for d in range(1, 4):
        partners += [to_x(d), to_y(d), to_g(d)]
    for to in partners:
        pl.semaphore_signal(barrier, inc=1, device_id=to, device_id_type=pl.DeviceIdType.MESH)
    read_w1 = pltpu.make_async_copy(w1, own, loc.at[0])
    read_h1 = pltpu.make_async_copy(h1, h1v, loc.at[1])
    read_w2 = pltpu.make_async_copy(w2t, w2tv, loc.at[2])
    read_h2 = pltpu.make_async_copy(h2, h2v, loc.at[3])
    read_counts = pltpu.make_async_copy(counts, cnt, loc.at[4])
    for read in (read_w1, read_h1, read_w2, read_h2, read_counts):
        read.start()
    read_w1.wait()
    pl.semaphore_wait(barrier, len(partners))

    go_z = copy(own, own, "z", 0, z_pair)
    go_z.start()
    read_h1.wait()
    hl[...] = h1v[...].astype(BF16)
    num[...] = jnp.zeros_like(num)
    cs[...] = jnp.zeros_like(cs)
    go_z.wait_recv()

    def stage_two(h, d):
        src = wg.at[mx, my, :, mc, h]
        return copy(src, src, "a2", 3 * h + d - 1, to_x(d) if h == 0 else to_y(d))

    for d in ORDER:
        for h in range(2):
            stage_two(h, d).start()
    for d in ORDER:
        for h in range(2):
            stage_two(h, d).wait_recv()

    def column(h, d):
        return wg.at[:, at_y(4 - d), :, mc, 0] if h == 0 else wg.at[at_x(4 - d), :, :, mc, 1]

    def stage_three(h, d):
        src = column(h, 0)
        return copy(src, src, "a3", 3 * h + d - 1, to_y(d) if h == 0 else to_x(d))

    def forward(h, d):
        src = column(h, d)
        return copy(src, src, "f", 4 * h + d, sibling)

    for d in ORDER:
        for h in range(2):
            stage_three(h, d).start()
    for h in range(2):
        forward(h, 0).start()

    read_counts.wait()

    def pass_on(d):
        for h in range(2):
            stage_three(h, d).wait_recv()
            forward(h, d).start()

    def first(w, v):
        approx = jnp.dot(w, hl[...], preferred_element_type=F32)
        ratio = (v.astype(F32) / approx).astype(BF16)
        add = lax.dot_general(
            w, ratio, (((0,), (0,)), ((), ())), preferred_element_type=F32
        )
        for j in range(NG):
            num[j] += add[:, j * 128 : (j + 1) * 128]
        cs[...] += jnp.sum(w.astype(F32).reshape(-1, 8, w.shape[1]), axis=0)

    def first_step(t, carry):
        d = t + t // 2 - 2 * (t // 3)
        forward(0, d).wait_recv()
        first(
            wg[:, at_y(4 - d), :, :, 0].reshape(512, 512),
            cnt[:, at_y(4 - d), :, :, 0].reshape(512, 512),
        )
        forward(1, d).wait_recv()
        first(
            wg[at_x(4 - d), :, :, :, 1].reshape(512, 512),
            cnt[at_x(4 - d), :, :, :, 1].reshape(512, 512),
        )

        @pl.when(t == 0)
        def _():
            pass_on(1)
            pass_on(3)

        @pl.when(t == 1)
        def _():
            pass_on(2)

        return carry

    lax.fori_loop(0, 4, first_step, 0)

    def send_num(d):
        return copy(nq.at[d - 1], nqr.at[d - 1], "n", d - 1, to_g(d))

    def send_marks(d):
        return copy(nm.at[d - 1], nmr.at[d - 1], "m", d - 1, to_g(d))

    for d in ORDER:
        q, most = coded(num[at_g(d)], 0)
        nq[d - 1] = q
        send_num(d).start()
        nm[d - 1, :, 0:512] = cs[...]
        nm[d - 1, :, 512:640] = jnp.broadcast_to(most, (8, 128))
        send_marks(d).start()
    read_w2.wait()
    read_h2.wait()
    w2 = jnp.transpose(w2tv[...])
    mine = pl.ds(pl.multiple_of(g * 128, 128), 128)
    h2_mine = h2v[:, mine]
    fit = high(w2, h2_mine)
    for d in ORDER:
        send_marks(d).wait_recv()
    parts = cs[...] + nmr[0, :, 0:512] + nmr[1, :, 0:512] + nmr[2, :, 0:512]
    total = jnp.sum(parts, axis=0, keepdims=True)
    colsum = jnp.transpose(jnp.broadcast_to(total, (128, 512)))
    h1_num = num[g]
    for d in ORDER:
        send_num(d).wait_recv()
        h1_num += decoded(nqr[d - 1], nmr[d - 1, 0:1, 512:640])
    fresh = h1v[:, mine] * h1_num / colsum
    top = fresh.astype(BF16)
    hbuf[0, g] = top
    hbuf[1, g] = (fresh - top.astype(F32)).astype(BF16)

    def send_h(h, d):
        src = hbuf.at[h, g]
        return copy(src, src, "hb", 3 * h + d - 1, to_g(d))

    for d in ORDER:
        send_h(0, d).start()

    ratio3 = fresh / fit
    lift = high(w2tv[...], ratio3)
    h2_new = h2_mine * lift / jnp.sum(w2tv[...], axis=1, keepdims=True)
    h2b[g] = h2_new
    ratio4 = fresh / high(w2, h2_new)
    w2_part = nt(h2_new, ratio4, HI)
    h2_part = jnp.broadcast_to(jnp.sum(h2_new, axis=1, keepdims=True), (64, 128))
    rows = nt(jnp.ones((8, 128), F32), fresh, HI)
    for j in range(NG):
        for c in range(NC):
            at = 16 * j + 8 * c
            sm[j, c, :, 0:512] = w2_part[at : at + 8]
            sm[j, c, :, 512:640] = h2_part[at : at + 8]
            sm[j, c, :, 640:768] = jnp.zeros((8, 128), F32)
            for k in range(4):
                sm[j, c, k : k + 1, 640:768] = rows[0:1, k * 128 : (k + 1) * 128]

    def sum_g(d):
        return copy(sm.at[at_g(d)], smr.at[d - 1], "s0", d - 1, to_g(d))

    sum_c = copy(sv.at[oc], svr, "s1", 0, sibling)
    sum_z = copy(sz, szr, "s2", 0, z_pair)

    def sum_x(d):
        return copy(sx.at[mx], sx.at[mx], "s3", d - 1, to_x(d))

    def sum_y(d):
        return copy(sy.at[my], sy.at[my], "s4", d - 1, to_y(d))

    def all_g(d):
        return copy(sg.at[mc, g], sg.at[mc, g], "s5", d - 1, to_g(d))

    all_c = copy(sg.at[mc], sg.at[mc], "s6", 0, sibling)

    def send_h2(d):
        return copy(h2b.at[g], h2b.at[g], "h2", d - 1, to_g(d))

    for d in ORDER:
        sum_g(d).start()
    for d in ORDER:
        send_h2(d).start()
    for d in ORDER:
        send_h(0, d).wait_recv()
    for j in range(NG):
        hl[:, j * 128 : (j + 1) * 128] = hbuf[0, j]

    def second(w, v):
        approx = jnp.dot(w, hl[...], preferred_element_type=F32)
        ratio = (v.astype(F32) / approx).astype(BF16)
        return nt(ratio, hl[...]).reshape(4, 2, 32, 512)

    def pick(ref, h, i, c):
        d = i + 1
        found = ref[at_x(d), :, :, c, 0] if h == 0 else ref[:, at_y(d), :, c, 1]
        return found.reshape(256, 512)

    def to_sibling(h, i):
        return copy(e1s.at[h, i], e1r.at[h, i], "e1", 4 * h + i, sibling)

    def along(h, i):
        to = to_x(i + 1) if h == 0 else to_y(i + 1)
        return (
            copy(pq.at[h, i], pqr.at[h, i], "p", 3 * h + i, to),
            copy(ps.at[h, i], psr.at[h, i], "ps", 3 * h + i, to),
        )

    def second_step(i, carry):
        for h in range(2):
            e1s[h, i] = second(pick(wg, h, i, oc), pick(cnt, h, i, oc))
            to_sibling(h, i).start()
        for h in range(2):
            part[h] = second(pick(wg, h, i, mc), pick(cnt, h, i, mc))
        for h in range(2):
            to_sibling(h, i).wait_recv()

            @pl.when(i < 3)
            def _():
                q, most = coded((part[h] + e1r[h, i]).reshape(8, 32, 512), 1)
                pq[h, i] = q.reshape(4, 2, 32, 512)
                ps[h, i] = most.reshape(8, 512)
                for go in along(h, i):
                    go.start()

            @pl.when(i == 3)
            def _():
                acc[h] = part[h] + e1r[h, 3]

        @pl.when(i == 0)
        def _():
            for d in ORDER:
                sum_g(d).wait_recv()
            sv[...] = sm[g] + smr[0] + smr[1] + smr[2]
            sum_c.start()
            for d in ORDER:
                send_h(1, d).start()

        @pl.when(i == 1)
        def _():
            sum_c.wait_recv()
            sz[...] = sv[mc] + svr[...]
            sum_z.start()

        @pl.when(i == 2)
        def _():
            sum_z.wait_recv()
            sx[mx] = sz[...] + szr[...]
            for d in ORDER:
                sum_x(d).start()

        @pl.when(i == 3)
        def _():
            for d in ORDER:
                sum_x(d).wait_recv()
            sy[my] = sx[0] + sx[1] + sx[2] + sx[3]
            for d in ORDER:
                sum_y(d).start()

        return carry

    lax.fori_loop(0, 4, second_step, 0)

    def across(h, d):
        to = to_y(d) if h == 0 else to_x(d)
        k = 3 * h + d - 1
        return (
            copy(aq.at[h, d - 1], aqr.at[h, d - 1], "q", k, to),
            copy(aps.at[h, d - 1], apr.at[h, d - 1], "qs", k, to),
        )

    for h in range(2):
        for i in (0, 2, 1):
            for go in along(h, i):
                go.wait_recv()
        whole = acc[h].reshape(8, 32, 512)
        for i in range(3):
            whole += decoded(pqr[h, i].reshape(8, 32, 512), psr[h, i].reshape(8, 1, 512))
        acc[h] = whole.reshape(4, 2, 32, 512)
        for d in ORDER:
            q, most = coded(acc[h, at_y(d) if h == 0 else at_x(d)], 1)
            aq[h, d - 1] = q
            aps[h, d - 1] = jnp.broadcast_to(most, (2, 8, 512))
            for go in across(h, d):
                go.start()
    for d in ORDER:
        sum_y(d).wait_recv()
    done = sy[0] + sy[1] + sy[2] + sy[3]
    sg[mc, g] = done
    for d in ORDER:
        all_g(d).start()
    for h in range(2):
        for d in ORDER:
            for go in across(h, d):
                go.wait_recv()
        whole = acc[h, my if h == 0 else mx]
        for k in range(3):
            whole += decoded(aqr[h, k], apr[h, k, :, 0:1])
        fin[:, h] = whole
    q, most = coded(fin[oz], 1)
    lq[...] = q
    lps[...] = jnp.broadcast_to(most, (2, 8, 512))
    last = (copy(lq, lqr, "l", 0, z_pair), copy(lps, lpr, "ls", 0, z_pair))
    for go in last:
        go.start()
    for d in ORDER:
        all_g(d).wait_recv()
    all_c.start()
    rowsum = jnp.concatenate([done[k : k + 1, 640:768] for k in range(4)], axis=1)
    for go in last:
        go.wait_recv()
    w1_num = (fin[mz] + decoded(lqr[...], lpr[:, 0:1])).reshape(64, 512)
    w1_now = wg[mx, my, mz, mc].astype(F32).reshape(64, 512)
    w1_out[...] = (w1_now * w1_num / rowsum).astype(BF16)
    all_c.wait_recv()
    for j in range(NG):
        for c in range(NC):
            at = slice(16 * j + 8 * c, 16 * j + 8 * c + 8)
            w2t_out[at, :] = w2tv[at, :] * sg[c, j, :, 0:512] / sg[c, j, :, 512:513]

    for d in ORDER:
        send_h(1, d).wait_recv()
        send_h2(d).wait_recv()
    for sent in (go_z, sum_c, sum_z, all_c) + last:
        sent.wait_send()
    for d in ORDER:
        for h in range(2):
            for sent in (stage_two(h, d), stage_three(h, d), send_h(h, d)):
                sent.wait_send()
            for sent in along(h, d - 1) + across(h, d):
                sent.wait_send()
        for sent in (send_num, send_marks, send_h2, sum_g, sum_x, sum_y, all_g):
            sent(d).wait_send()
    for h in range(2):
        for d in range(4):
            forward(h, d).wait_send()
            to_sibling(h, d).wait_send()


def finish(w1, hbuf, w2t, h2b, w1_out, h1_out, w2t_out, h2_out):
    w1_out[...] = w1[...]
    w2t_out[...] = w2t[...]
    for j in range(NG):
        at = slice(j * 128, (j + 1) * 128)
        h1_out[:, at] = hbuf[0, j].astype(F32) + hbuf[1, j].astype(F32)
        h2_out[:, at] = h2b[j]


def on_device(counts, w1, h1, w2, h2):
    vmem = pl.BlockSpec(memory_space=pltpu.VMEM)
    shape = (NX, NY, NZ, NC, 2, 32, 512)
    sds = jax.ShapeDtypeStruct
    scratch = [
        (shape, BF16), (shape, jnp.int32), ((512, 512), F32), ((64, 512), F32), ((64, 512), F32),
        ((512, 512), BF16), ((NG, 512, 128), F32), ((3, 512, 128), I16), ((3, 512, 128), I16),
        ((3, 8, 640), F32), ((3, 8, 640), F32), ((8, 512), F32),
        ((2, 4, 4, 2, 32, 512), F32), ((2, 4, 4, 2, 32, 512), F32),
        ((2, 4, 2, 32, 512), F32), ((2, 4, 2, 32, 512), F32),
        ((2, 3, 4, 2, 32, 512), I16), ((2, 3, 4, 2, 32, 512), I16), ((2, 3, 8, 512), F32), ((2, 3, 8, 512), F32),
        ((2, 3, 2, 32, 512), I16), ((2, 3, 2, 32, 512), I16), ((2, 3, 2, 8, 512), F32), ((2, 3, 2, 8, 512), F32),
        ((2, 2, 32, 512), F32), ((2, 32, 512), I16), ((2, 32, 512), I16), ((2, 8, 512), F32), ((2, 8, 512), F32),
        ((NG, 2, 8, 768), F32), ((3, 2, 8, 768), F32), ((2, 8, 768), F32), ((8, 768), F32),
        ((8, 768), F32), ((8, 768), F32), ((4, 8, 768), F32), ((4, 8, 768), F32), ((2, NG, 8, 768), F32),
    ]
    moved = pl.pallas_call(
        kernel,
        out_shape=(
            sds((64, 512), BF16),
            sds((2, NG, 512, 128), BF16),
            sds((64, 512), F32),
            sds((NG, 64, 128), F32),
        ),
        in_specs=[pl.BlockSpec(memory_space=pl.ANY)] * 5,
        out_specs=(vmem,) * 4,
        scratch_shapes=[pltpu.VMEM(*s) for s in scratch]
        + [
            pltpu.SemaphoreType.DMA((S_ALL,)),
            pltpu.SemaphoreType.DMA((S_ALL,)),
            pltpu.SemaphoreType.DMA((5,)),
        ],
        compiler_params=pltpu.CompilerParams(
            collective_id=0, has_side_effects=True, vmem_limit_bytes=56 * 1024 * 1024
        ),
    )(counts.reshape(shape), w1.reshape(2, 32, 512), h1, w2.T, h2)
    w1_new, h1_new, w2t_new, h2_new = pl.pallas_call(
        finish,
        out_shape=(
            sds((64, 512), BF16),
            sds((512, 512), F32),
            sds((64, 512), F32),
            sds((64, 512), F32),
        ),
        in_specs=[vmem] * 4,
        out_specs=(vmem,) * 4,
    )(*moved)
    return w1_new, h1_new, w2t_new.T, h2_new


def solution(mesh):
    placed = (P("gene", "cell"), P(("gene", "cell"), None), P(None, "cell"), P(), P(None, "cell"))
    return jax.shard_map(
        on_device,
        mesh=mesh,
        in_specs=placed,
        out_specs=(P(("gene", "cell"), None), P(None, "cell"), P(), P(None, "cell")),
        check_vma=False,
    )
```

time: 999 us -> 107 us (0.11)
  waiting for transfers between devices: 795 us -> 0 us
  blocking collectives: 148 us -> 0 us
  Pallas kernels: 0 us -> 106 us
  matrix products: 30.7 us -> 0 us
  between operations: 13.8 us -> 0.64 us
    psum x2 -> x0, waiting for transfers between devices: 384 us -> none  [the longest x1 331 us: on_device(): w2_num, h2_rows = lax.psum((w2_part, h2_part), 'cell')]
    reduce_scatter x1 -> x0, waiting for transfers between devices: 296 us -> none  [on_device(): lax.psum_scatter(lax.dot_general(ratio2, h1_low2, (((1,), (1,)), ((), ())...]
    psum x2 -> x0, blocking collectives: 148 us -> none  [the longest x1 138 us: on_device(): rowsum = lax.psum(local_rows, 'cell')]
    all_gather x1 -> x0, waiting for transfers between devices: 115 us -> none  [on_device(): w1_block = lax.all_gather(w1, 'cell', axis=0, tiled=True)]
    pallas_call x0 -> x2, Pallas kernels: none -> 106 us  [the longest x1 104 us: on_device(): pl.pallas_call(kernel, out_shape=(sds((64, 512), BF16), sds((2, NG, 512,...]
    dot_general x6 -> x0, matrix products: 30.7 us -> none  [the longest x1 12.5 us: on_device(): lax.dot_general(ratio2, h1_low2, (((1,), (1,)), ((), ())), preferred_elem...]
  transfers between devices with their start and end apart: 4 -> 0, of which waited for: 4 -> 0; matrix products, arithmetic and copies ran while one was open for 2% -> 0% of each run, Pallas kernels for 0% -> 0%
where the time goes in v2:
time: 107 us
  Pallas kernels  106 us (99%)
    pallas_call x1, Pallas kernels, on_device(): pl.pallas_call(kernel, out_shape=(sds((64, 512), BF16), sds((2, NG, 512,...  104 us
    pallas_call x1, Pallas kernels, on_device(): pl.pallas_call(finish, out_shape=(sds((64, 512), BF16), sds((512, 512), F...  2.45 us

profile of v2, /device:TPU:1, one launch (start us, length us, event | category | flops | bytes accessed | tf_op | source)
XLA Modules:
  0.0 107.0 jit_solution(10208116213547421361)
XLA Ops:
  0.6 103.9 %shard_map.84 = (bf16[64,512]{1,0:T(8,128)(2,1)}, bf16[2,4,512,128]{3,2,1,0:T(8,128)(2,1)}, f32[64,512]{1,0:T(8,128)}, f32[4,64,128]{2,1,0:T(8,128)}) custom-call(s32[4,4,2,2,2,32,512]{6,5,4,3,2,1,0:T(8,128)} %bitcast.4, bf16[2,32,512]{2,1,0:T(8,128)(2,1)} %bitcast.6, f32[512,512]{1,0:T(8,128)} %h1.1, f32[64,512]{1,0:T(8,128)} %bitcast.5, f32[64,512]{1,0:T(8,128)} %h2.1), custom_call_target="tpu_custom_call" | custom-call | tf_op jit(solution)/shard_map/pallas_call | solution.py:450
  104.6 2.5 %shard_map.85 = (bf16[64,512]{1,0:T(8,128)(2,1)}, f32[512,512]{1,0:T(8,128)}, f32[64,512]{1,0:T(8,128)}, f32[64,512]{1,0:T(8,128)}) custom-call(bf16[64,512]{1,0:T(8,128)(2,1)} %get-tuple-element.12.w1, bf16[2,4,512,128]{3,2,1,0:T(8,128)(2,1)} %get-tuple-element.13.hbuf, f32[64,512]{1,0:T(8,128)} %get-tuple-element.14.w2t, f32[4,64,128]{2,1,0:T(8,128)} %get-tuple-element.15.h2b), custom_call_target="tpu_custom_call" | custom-call | tf_op jit(solution)/shard_map/pallas_call | solution.py:470

commit v3 on v2

v3 whole, which is shorter than its diff:
```python
import jax
import jax.numpy as jnp
from jax import lax
from jax.experimental import pallas as pl
from jax.experimental.pallas import tpu as pltpu
from jax.sharding import PartitionSpec as P

NX, NY, NZ, NC = 4, 4, 2, 2
NG = 4
F32, BF16, I16 = jnp.float32, jnp.bfloat16, jnp.int16
HI = lax.Precision.HIGHEST
TOP = 32767.0
ORDER = (1, 3, 2)

SIZES = dict(
    z=1, a2=12, a3=18, f=8, m=3, n=6, hb=6, hs=6, h2=3, e1=8, p=6, ps=6, q=6, qs=6, l=1, ls=1,
    s0=1, s1=3, s2=1, s3=3, s4=3, s5=3, s6=1,
)
PLACE, S_ALL = {}, 0
for _name, _size in SIZES.items():
    PLACE[_name] = S_ALL
    S_ALL += _size


def nt(a, b, precision=None):
    return lax.dot_general(
        a, b, (((1,), (1,)), ((), ())), preferred_element_type=F32, precision=precision
    )


def high(a, b):
    return jnp.dot(a, b, precision=HI, preferred_element_type=F32)


def most_of(v, axis):
    return jnp.maximum(jnp.max(v, axis=axis, keepdims=True), 1e-30)


def coded(v, most):
    return jnp.round(v * (TOP / most)).astype(jnp.int32).astype(I16)


def decoded(q, most):
    return q.astype(jnp.int32).astype(F32) * (most * (1.0 / TOP))


def kernel(
    counts, w1, h1, w2t, h2,
    w1_out, h1_out, w2t_out, h2_out,
    wg, cnt, h1v, w2tv, h2v, hl, num, nq, nqr, nm, nmr, cs, fr, hq, hs, h1f, h2b,
    rb, e1r, acc, pq, pqr, ps, psr, aq, aqr, aps, apr, fin, lq, lqr, lps, lpr,
    sm, smr, sv, svr, sz, szr, sx, sy, sg, w1f, w2f,
    snd, rcv, loc,
):
    g = lax.axis_index("gene")
    ci = lax.axis_index("cell")
    mx, my, mz, mc = ci // 16, (ci // 4) % 4, (ci // 2) % 2, ci % 2
    oz, oc = 1 - mz, 1 - mc

    def cell(x, y, z, c):
        return ((x * NY + y) * NZ + z) * NC + c

    def at_x(d):
        return (mx + d) % NX

    def at_y(d):
        return (my + d) % NY

    def at_g(d):
        return (g + d) % NG

    def copy(src, dst, name, k, to):
        sem = PLACE[name] + k
        return pltpu.make_async_remote_copy(
            src_ref=src,
            dst_ref=dst,
            send_sem=snd.at[sem],
            recv_sem=rcv.at[sem],
            device_id=to,
            device_id_type=pl.DeviceIdType.MESH,
        )

    sibling = (g, cell(mx, my, mz, oc))
    z_pair = (g, cell(mx, my, oz, mc))

    def to_x(d):
        return (g, cell(at_x(d), my, mz, mc))

    def to_y(d):
        return (g, cell(mx, at_y(d), mz, mc))

    def to_g(d):
        return (at_g(d), ci)

    own = wg.at[mx, my, mz, mc]
    barrier = pltpu.get_barrier_semaphore()
    partners = [sibling, z_pair]
    for d in range(1, 4):
        partners += [to_x(d), to_y(d), to_g(d)]
    for to in partners:
        pl.semaphore_signal(barrier, inc=1, device_id=to, device_id_type=pl.DeviceIdType.MESH)
    read_w1 = pltpu.make_async_copy(w1, own, loc.at[0])
    read_h1 = pltpu.make_async_copy(h1, h1v, loc.at[1])
    read_w2 = pltpu.make_async_copy(w2t, w2tv, loc.at[2])
    read_h2 = pltpu.make_async_copy(h2, h2v, loc.at[3])
    read_counts = pltpu.make_async_copy(counts, cnt, loc.at[4])
    for read in (read_w1, read_h1, read_w2, read_h2, read_counts):
        read.start()
    read_w1.wait()
    pl.semaphore_wait(barrier, len(partners))

    go_z = copy(own, own, "z", 0, z_pair)
    go_z.start()

    def near(k, a, d):
        src = wg.at[mx, my, oz if k else mz, mc]
        return copy(src, src, "a2", 6 * k + 3 * a + d - 1, to_y(d) if a else to_x(d))

    for d in ORDER:
        for a in range(2):
            near(0, a, d).start()
    read_h1.wait()
    hl[...] = h1v[...].astype(BF16)
    num[...] = jnp.zeros_like(num)
    cs[...] = jnp.zeros_like(cs)
    go_z.wait_recv()
    for d in ORDER:
        for a in range(2):
            near(1, a, d).start()

    def column(h, d):
        return wg.at[:, at_y(4 - d), :, mc, 0] if h == 0 else wg.at[at_x(4 - d), :, :, mc, 1]

    def far(h, e, d):
        src = wg.at[mx, at_y(4 - e), :, mc, 1] if h else wg.at[at_x(4 - e), my, :, mc, 0]
        return copy(src, src, "a3", 9 * h + 3 * (e - 1) + d - 1, to_x(d) if h else to_y(d))

    def forward(h, d):
        src = column(h, d)
        return copy(src, src, "f", 4 * h + d, sibling)

    for e in ORDER:
        for h in range(2):
            near(0, h, e).wait_recv()
            near(1, h, e).wait_recv()
            for d in ORDER:
                far(h, e, d).start()
    for h in range(2):
        forward(h, 0).start()

    read_counts.wait()

    def pass_on(d):
        for h in range(2):
            for e in ORDER:
                far(h, e, d).wait_recv()
            forward(h, d).start()

    def first(w, v):
        approx = jnp.dot(w, hl[...], preferred_element_type=F32)
        ratio = (v.astype(F32) / approx).astype(BF16)
        add = lax.dot_general(
            w, ratio, (((0,), (0,)), ((), ())), preferred_element_type=F32
        )
        for j in range(NG):
            num[j] += add[:, j * 128 : (j + 1) * 128]
        cs[...] += jnp.sum(w.astype(F32).reshape(-1, 8, w.shape[1]), axis=0)

    def first_step(t, carry):
        d = t + t // 2 - 2 * (t // 3)
        forward(0, d).wait_recv()
        first(
            wg[:, at_y(4 - d), :, :, 0].reshape(512, 512),
            cnt[:, at_y(4 - d), :, :, 0].reshape(512, 512),
        )
        forward(1, d).wait_recv()
        first(
            wg[at_x(4 - d), :, :, :, 1].reshape(512, 512),
            cnt[at_x(4 - d), :, :, :, 1].reshape(512, 512),
        )

        @pl.when(t == 0)
        def _():
            pass_on(1)
            pass_on(3)

        @pl.when(t == 1)
        def _():
            pass_on(2)

        return carry

    lax.fori_loop(0, 4, first_step, 0)

    def block(b):
        return pl.ds(256 * b, 256)

    def send_num(b, d):
        return copy(nq.at[d - 1, block(b)], nqr.at[d - 1, block(b)], "n", 3 * b + d - 1, to_g(d))

    def send_marks(d):
        return copy(nm.at[d - 1], nmr.at[d - 1], "m", d - 1, to_g(d))

    def send_h(b, d):
        k = 3 * b + d - 1
        return (
            copy(hq.at[b, g], hq.at[b, g], "hb", k, to_g(d)),
            copy(hs.at[b, g], hs.at[b, g], "hs", k, to_g(d)),
        )

    for d in ORDER:
        most = most_of(num[at_g(d)], 0)
        nm[d - 1, :, 0:512] = cs[...]
        nm[d - 1, :, 512:640] = jnp.broadcast_to(most, (8, 128))
        send_marks(d).start()
        nq[d - 1, 0:256] = coded(num[at_g(d), 0:256], most)
        send_num(0, d).start()
    for d in ORDER:
        nq[d - 1, 256:512] = coded(num[at_g(d), 256:512], nm[d - 1, 0:1, 512:640])
        send_num(1, d).start()
    read_w2.wait()
    read_h2.wait()
    w2 = jnp.transpose(w2tv[...])
    mine = pl.ds(pl.multiple_of(g * 128, 128), 128)
    h2_mine = h2v[:, mine]
    fit = high(w2, h2_mine)
    for d in ORDER:
        send_marks(d).wait_recv()
    parts = cs[...] + nmr[0, :, 0:512] + nmr[1, :, 0:512] + nmr[2, :, 0:512]
    total = jnp.sum(parts, axis=0, keepdims=True)
    colsum = jnp.transpose(jnp.broadcast_to(total, (128, 512)))
    for b in range(2):
        at = slice(256 * b, 256 * b + 256)
        h1_num = num[g, at]
        for d in ORDER:
            send_num(b, d).wait_recv()
            h1_num += decoded(nqr[d - 1, at], nmr[d - 1, 0:1, 512:640])
        new = h1v[at, mine] * h1_num / colsum[at]
        fr[at] = new
        most = most_of(new, 0)
        hq[b, g] = coded(new, most)
        hs[b, g] = jnp.broadcast_to(most, (8, 128))
        for d in ORDER:
            for go in send_h(b, d):
                go.start()
    fresh = fr[...]

    ratio3 = fresh / fit
    lift = high(w2tv[...], ratio3)
    h2_new = h2_mine * lift / jnp.sum(w2tv[...], axis=1, keepdims=True)
    h2b[g] = h2_new
    ratio4 = fresh / high(w2, h2_new)
    w2_part = nt(h2_new, ratio4, HI)
    h2_part = jnp.broadcast_to(jnp.sum(h2_new, axis=1, keepdims=True), (64, 128))
    rows = nt(jnp.ones((8, 128), F32), fresh, HI)
    for j in range(NG):
        for c in range(NC):
            at = 16 * j + 8 * c
            sm[c, j, :, 0:512] = w2_part[at : at + 8]
            sm[c, j, :, 512:640] = h2_part[at : at + 8]
            sm[c, j, :, 640:768] = jnp.zeros((8, 128), F32)
            for k in range(4):
                sm[c, j, k : k + 1, 640:768] = rows[0:1, k * 128 : (k + 1) * 128]

    sum_c = copy(sm.at[oc], smr, "s0", 0, sibling)

    def sum_g(d):
        return copy(sv.at[at_g(d)], svr.at[d - 1], "s1", d - 1, to_g(d))

    sum_z = copy(sz, szr, "s2", 0, z_pair)

    def sum_x(d):
        return copy(sx.at[mx], sx.at[mx], "s3", d - 1, to_x(d))

    def sum_y(d):
        return copy(sy.at[my], sy.at[my], "s4", d - 1, to_y(d))

    def all_g(d):
        return copy(sg.at[mc, g], sg.at[mc, g], "s5", d - 1, to_g(d))

    all_c = copy(sg.at[mc], sg.at[mc], "s6", 0, sibling)

    def send_h2(d):
        return copy(h2b.at[g], h2b.at[g], "h2", d - 1, to_g(d))

    sum_c.start()
    for b in range(2):
        for d in (0,) + ORDER:
            if d:
                for go in send_h(b, d):
                    go.wait_recv()
            j = at_g(4 - d)
            value = decoded(hq[b, j], hs[b, j, 0:1])
            there = pl.ds(pl.multiple_of(j * 128, 128), 128)
            h1f[block(b), there] = value
            hl[block(b), there] = value.astype(BF16)
        if b == 0:
            sum_c.wait_recv()
            sv[...] = sm[mc] + smr[...]
            for d in ORDER:
                sum_g(d).start()

    def second(h, i):
        d = i + 1
        w = wg[:, at_y(d), :, :, 1] if h else wg[at_x(d), :, :, :, 0]
        v = cnt[:, at_y(d), :, :, 1] if h else cnt[at_x(d), :, :, :, 0]
        approx = jnp.dot(w.reshape(512, 512), hl[...], preferred_element_type=F32)
        ratio = (v.reshape(512, 512).astype(F32) / approx).astype(BF16)
        rb[h, i] = nt(ratio, hl[...]).reshape(4, 2, 2, 32, 512)

    def to_sibling(h, i):
        return copy(rb.at[h, i, :, :, oc], e1r.at[h, i], "e1", 4 * h + i, sibling)

    def along(h, i):
        to = to_x(i + 1) if h == 0 else to_y(i + 1)
        return (
            copy(pq.at[h, i], pqr.at[h, i], "p", 3 * h + i, to),
            copy(ps.at[h, i], psr.at[h, i], "ps", 3 * h + i, to),
        )

    def add_up(h, i):
        to_sibling(h, i).wait_recv()
        both = rb[h, i, :, :, mc] + e1r[h, i]

        @pl.when(i < 3)
        def _():
            v = both.reshape(8, 32, 512)
            most = most_of(v, 1)
            pq[h, i] = coded(v, most).reshape(4, 2, 32, 512)
            ps[h, i] = most.reshape(8, 512)
            for go in along(h, i):
                go.start()

        @pl.when(i == 3)
        def _():
            acc[h] = both

    def second_step(i, carry):
        @pl.when(i < 4)
        def _():
            for h in range(2):
                second(h, i)
                to_sibling(h, i).start()

        @pl.when(i > 0)
        def _():
            for h in range(2):
                add_up(h, i - 1)

        @pl.when(i == 2)
        def _():
            for d in ORDER:
                sum_g(d).wait_recv()
            sz[...] = sv[g] + svr[0] + svr[1] + svr[2]
            sum_z.start()
            for d in ORDER:
                send_h2(d).start()

        @pl.when(i == 4)
        def _():
            sum_z.wait_recv()
            sx[mx] = sz[...] + szr[...]
            for d in ORDER:
                sum_x(d).start()

        return carry

    lax.fori_loop(0, 5, second_step, 0)
    put_h1 = pltpu.make_async_copy(h1f, h1_out, loc.at[5])
    put_h1.start()

    def across(h, d):
        to = to_y(d) if h == 0 else to_x(d)
        k = 3 * h + d - 1
        return (
            copy(aq.at[h, d - 1], aqr.at[h, d - 1], "q", k, to),
            copy(aps.at[h, d - 1], apr.at[h, d - 1], "qs", k, to),
        )

    for h in range(2):
        for i in (0, 2, 1):
            for go in along(h, i):
                go.wait_recv()
        whole = acc[h].reshape(8, 32, 512)
        for i in range(3):
            whole += decoded(pqr[h, i].reshape(8, 32, 512), psr[h, i].reshape(8, 1, 512))
        acc[h] = whole.reshape(4, 2, 32, 512)
        for d in ORDER:
            v = acc[h, at_y(d) if h == 0 else at_x(d)]
            most = most_of(v, 1)
            aq[h, d - 1] = coded(v, most)
            aps[h, d - 1] = jnp.broadcast_to(most, (2, 8, 512))
            for go in across(h, d):
                go.start()
    for d in ORDER:
        sum_x(d).wait_recv()
    sy[my] = sx[0] + sx[1] + sx[2] + sx[3]
    for d in ORDER:
        sum_y(d).start()
    for d in ORDER:
        sum_y(d).wait_recv()
    done = sy[0] + sy[1] + sy[2] + sy[3]
    sg[mc, g] = done
    for d in ORDER:
        all_g(d).start()
    for h in range(2):
        for d in ORDER:
            for go in across(h, d):
                go.wait_recv()
        whole = acc[h, my if h == 0 else mx]
        for k in range(3):
            whole += decoded(aqr[h, k], apr[h, k, :, 0:1])
        fin[:, h] = whole
    most = most_of(fin[oz], 1)
    lq[...] = coded(fin[oz], most)
    lps[...] = jnp.broadcast_to(most, (2, 8, 512))
    last = (copy(lq, lqr, "l", 0, z_pair), copy(lps, lpr, "ls", 0, z_pair))
    for go in last:
        go.start()
    for d in ORDER:
        all_g(d).wait_recv()
    all_c.start()
    for d in ORDER:
        send_h2(d).wait_recv()
    puts = [
        pltpu.make_async_copy(h2b.at[j], h2_out.at[:, 128 * j : 128 * j + 128], loc.at[6 + j])
        for j in range(NG)
    ]
    for put in puts:
        put.start()
    rowsum = jnp.concatenate([done[k : k + 1, 640:768] for k in range(4)], axis=1)
    for go in last:
        go.wait_recv()
    w1_num = (fin[mz] + decoded(lqr[...], lpr[:, 0:1])).reshape(64, 512)
    w1_now = wg[mx, my, mz, mc].astype(F32).reshape(64, 512)
    w1f[...] = (w1_now * w1_num / rowsum).astype(BF16)
    puts.append(pltpu.make_async_copy(w1f, w1_out, loc.at[10]))
    puts[-1].start()
    all_c.wait_recv()
    for j in range(NG):
        for c in range(NC):
            at = slice(16 * j + 8 * c, 16 * j + 8 * c + 8)
            w2f[at, :] = w2tv[at, :] * sg[c, j, :, 0:512] / sg[c, j, :, 512:513]

    puts.append(pltpu.make_async_copy(w2f, w2t_out, loc.at[11]))
    puts[-1].start()

    for sent in (go_z, sum_c, sum_z, all_c) + last:
        sent.wait_send()
    for d in ORDER:
        for h in range(2):
            for sent in (near(0, h, d), near(1, h, d), send_num(h, d)) + send_h(h, d):
                sent.wait_send()
            for e in ORDER:
                far(h, e, d).wait_send()
            for sent in along(h, d - 1) + across(h, d):
                sent.wait_send()
        for sent in (send_marks, send_h2, sum_g, sum_x, sum_y, all_g):
            sent(d).wait_send()
    for h in range(2):
        for d in range(4):
            forward(h, d).wait_send()
            to_sibling(h, d).wait_send()
    for put in puts + [put_h1]:
        put.wait()


def finish(*refs):
    *arrays, sem = refs
    copies = [
        pltpu.make_async_copy(arrays[k], arrays[k + 4], sem.at[k]) for k in range(4)
    ]
    for go in copies:
        go.start()
    for go in copies:
        go.wait()


def on_device(counts, w1, h1, w2, h2):
    anywhere = pl.BlockSpec(memory_space=pl.ANY)
    shape = (NX, NY, NZ, NC, 2, 32, 512)
    sds = jax.ShapeDtypeStruct
    outs = (
        sds((64, 512), BF16),
        sds((512, 512), F32),
        sds((64, 512), F32),
        sds((64, 512), F32),
    )
    scratch = [
        (shape, BF16), (shape, jnp.int32), ((512, 512), F32), ((64, 512), F32), ((64, 512), F32),
        ((512, 512), BF16), ((NG, 512, 128), F32), ((3, 512, 128), I16), ((3, 512, 128), I16),
        ((3, 8, 640), F32), ((3, 8, 640), F32), ((8, 512), F32),
        ((512, 128), F32), ((2, NG, 256, 128), I16), ((2, NG, 8, 128), F32), ((512, 512), F32), ((NG, 64, 128), F32),
        ((2, 4, 4, 2, 2, 32, 512), F32), ((2, 4, 4, 2, 32, 512), F32), ((2, 4, 2, 32, 512), F32),
        ((2, 3, 4, 2, 32, 512), I16), ((2, 3, 4, 2, 32, 512), I16), ((2, 3, 8, 512), F32), ((2, 3, 8, 512), F32),
        ((2, 3, 2, 32, 512), I16), ((2, 3, 2, 32, 512), I16), ((2, 3, 2, 8, 512), F32), ((2, 3, 2, 8, 512), F32),
        ((2, 2, 32, 512), F32), ((2, 32, 512), I16), ((2, 32, 512), I16), ((2, 8, 512), F32), ((2, 8, 512), F32),
        ((2, NG, 8, 768), F32), ((NG, 8, 768), F32), ((NG, 8, 768), F32), ((3, 8, 768), F32), ((8, 768), F32),
        ((8, 768), F32), ((4, 8, 768), F32), ((4, 8, 768), F32), ((2, NG, 8, 768), F32),
        ((64, 512), BF16), ((64, 512), F32),
    ]
    moved = pl.pallas_call(
        kernel,
        out_shape=outs,
        in_specs=[anywhere] * 5,
        out_specs=(anywhere,) * 4,
        scratch_shapes=[pltpu.VMEM(*s) for s in scratch]
        + [
            pltpu.SemaphoreType.DMA((S_ALL,)),
            pltpu.SemaphoreType.DMA((S_ALL,)),
            pltpu.SemaphoreType.DMA((12,)),
        ],
        compiler_params=pltpu.CompilerParams(
            collective_id=0, has_side_effects=True, vmem_limit_bytes=56 * 1024 * 1024
        ),
    )(counts.reshape(shape), w1.reshape(2, 32, 512), h1, w2.T, h2)
    w1_new, h1_new, w2t_new, h2_new = pl.pallas_call(
        finish,
        out_shape=outs,
        in_specs=[anywhere] * 4,
        out_specs=(anywhere,) * 4,
        scratch_shapes=[pltpu.SemaphoreType.DMA((4,))],
    )(*moved)
    return w1_new, h1_new, w2t_new.T, h2_new


def solution(mesh):
    placed = (P("gene", "cell"), P(("gene", "cell"), None), P(None, "cell"), P(), P(None, "cell"))
    return jax.shard_map(
        on_device,
        mesh=mesh,
        in_specs=placed,
        out_specs=(P(("gene", "cell"), None), P(None, "cell"), P(), P(None, "cell")),
        check_vma=False,
    )
```

time: 107 us -> 141 us (1.32)
  Pallas kernels: 106 us -> 140 us
    pallas_call x2, Pallas kernels: 106 us -> 140 us  [the longest x1 97.3 us: on_device(): pl.pallas_call(kernel, out_shape=outs, in_specs=[anywhere] * 5, out_specs...]
where the time goes in v3:
time: 141 us
  Pallas kernels  140 us (99%)
    pallas_call x1, Pallas kernels, on_device(): pl.pallas_call(kernel, out_shape=outs, in_specs=[anywhere] * 5, out_specs...  97.3 us
    pallas_call x1, Pallas kernels, on_device(): pl.pallas_call(finish, out_shape=outs, in_specs=[anywhere] * 4, out_specs...  42.8 us

profile of v3, /device:TPU:1, one launch (start us, length us, event | category | flops | bytes accessed | tf_op | source)
XLA Modules:
  0.0 140.8 jit_solution(3145821859773022013)
XLA Ops:
  0.6 97.3 %shard_map.84 = (bf16[64,512]{1,0:T(8,128)(2,1)}, f32[512,512]{1,0:T(8,128)}, f32[64,512]{1,0:T(8,128)}, f32[64,512]{1,0:T(8,128)}) custom-call(s32[4,4,2,2,2,32,512]{6,5,4,3,2,1,0:T(8,128)} %bitcast.4, bf16[2,32,512]{2,1,0:T(8,128)(2,1)} %bitcast.6, f32[512,512]{1,0:T(8,128)} %h1.1, f32[64,512]{1,0:T(8,128)} %bitcast.5, f32[64,512]{1,0:T(8,128)} %h2.1), custom_call_target="tpu_custom_call" | custom-call | tf_op jit(solution)/shard_map/pallas_call | solution.py:502
  98.0 42.8 %shard_map.85 = (bf16[64,512]{1,0:T(8,128)(2,1)}, f32[512,512]{1,0:T(8,128)}, f32[64,512]{1,0:T(8,128)}, f32[64,512]{1,0:T(8,128)}) custom-call(bf16[64,512]{1,0:T(8,128)(2,1)} %get-tuple-element.12.refs_0_, f32[512,512]{1,0:T(8,128)} %get-tuple-element.13.refs_1_, f32[64,512]{1,0:T(8,128)} %get-tuple-element.14.refs_2_, f32[64,512]{1,0:T(8,128)} %get-tuple-element.15.refs_3_), custom_call_target="tpu_custom_call" | custom-call | tf_op jit(solution)/shard_map/pallas_call | solution.py:517

commit v4 on v3

--- a/solution.py
+++ b/solution.py
@@ -13,7 +13,7 @@
 ORDER = (1, 3, 2)
 
 SIZES = dict(
-    z=1, a2=12, a3=18, f=8, m=3, n=6, hb=6, hs=6, h2=3, e1=8, p=6, ps=6, q=6, qs=6, l=1, ls=1,
+    z=1, a2=12, a3=18, f=8, m=3, nd=4, n=8, hb=4, hf=4, hs=6, h2=3, e1=8, p=6, ps=6, q=6, qs=6, l=1, ls=1,
     s0=1, s1=3, s2=1, s3=3, s4=3, s5=3, s6=1,
 )
 PLACE, S_ALL = {}, 0
@@ -192,32 +192,58 @@
 
     lax.fori_loop(0, 4, first_step, 0)
 
-    def block(b):
-        return pl.ds(256 * b, 256)
-
-    def send_num(b, d):
-        return copy(nq.at[d - 1, block(b)], nqr.at[d - 1, block(b)], "n", 3 * b + d - 1, to_g(d))
+    def rows(b, p):
+        return slice(256 * b + 128 * p, 256 * b + 128 * p + 128)
 
     def send_marks(d):
         return copy(nm.at[d - 1], nmr.at[d - 1], "m", d - 1, to_g(d))
 
+    def send_diag(b, p):
+        at = rows(b, p)
+        return copy(nq.at[1, at], nqr.at[1, at], "nd", 2 * b + p, to_g(3 if p else 1))
+
+    def send_num(b, d, p):
+        at = rows(b, p)
+        return copy(nq.at[d - 1, at], nqr.at[d - 1, at], "n", 4 * b + 2 * p + d // 3, to_g(d))
+
     def send_h(b, d):
-        k = 3 * b + d - 1
-        return (
-            copy(hq.at[b, g], hq.at[b, g], "hb", k, to_g(d)),
-            copy(hs.at[b, g], hs.at[b, g], "hs", k, to_g(d)),
-        )
-
-    for d in ORDER:
-        most = most_of(num[at_g(d)], 0)
+        return copy(hq.at[b, g], hq.at[b, g], "hb", 2 * b + d // 3, to_g(d))
+
+    def send_hs(b, d):
+        return copy(hs.at[b, g], hs.at[b, g], "hs", 3 * b + d - 1, to_g(d))
+
+    def pass_h(b, p):
+        src = hq.at[b, at_g(1 if p else 3), 128 * p : 128 * p + 128]
+        return copy(src, src, "hf", 2 * b + p, to_g(3 if p else 1))
+
+    far_most = most_of(num[at_g(2)], 0)
+    for d in (2, 1, 3):
+        most = far_most if d == 2 else most_of(num[at_g(d)], 0)
         nm[d - 1, :, 0:512] = cs[...]
         nm[d - 1, :, 512:640] = jnp.broadcast_to(most, (8, 128))
+        nm[d - 1, :, 640:768] = jnp.broadcast_to(far_most, (8, 128))
         send_marks(d).start()
-        nq[d - 1, 0:256] = coded(num[at_g(d), 0:256], most)
-        send_num(0, d).start()
-    for d in ORDER:
-        nq[d - 1, 256:512] = coded(num[at_g(d), 256:512], nm[d - 1, 0:1, 512:640])
-        send_num(1, d).start()
+
+    def code_num(b, d, p, more, most):
+        at = rows(b, p)
+        value = num[at_g(d), at]
+        if more is not None:
+            value += decoded(nqr[1, at], more)
+        nq[d - 1, at] = coded(value, most)
+
+    def mark(d):
+        return nm[d - 1, 0:1, 512:640]
+
+    def sent_mark(d, k=0):
+        return nmr[d - 1, 0:1, 512 + 128 * k : 640 + 128 * k]
+
+    for b in range(2):
+        for p in range(2):
+            code_num(b, 2, p, None, far_most)
+            send_diag(b, p).start()
+        for d, p in ((1, 1), (3, 0)):
+            code_num(b, d, p, None, mark(d))
+            send_num(b, d, p).start()
     read_w2.wait()
     read_h2.wait()
     w2 = jnp.transpose(w2tv[...])
@@ -226,23 +252,57 @@
     fit = high(w2, h2_mine)
     for d in ORDER:
         send_marks(d).wait_recv()
+    for b in range(2):
+        for d, p in ((1, 0), (3, 1)):
+            send_diag(b, p).wait_recv()
+            code_num(b, d, p, sent_mark(d, 1), mark(d) + sent_mark(d, 1))
+            send_num(b, d, p).start()
     parts = cs[...] + nmr[0, :, 0:512] + nmr[1, :, 0:512] + nmr[2, :, 0:512]
     total = jnp.sum(parts, axis=0, keepdims=True)
     colsum = jnp.transpose(jnp.broadcast_to(total, (128, 512)))
     for b in range(2):
-        at = slice(256 * b, 256 * b + 256)
-        h1_num = num[g, at]
-        for d in ORDER:
-            send_num(b, d).wait_recv()
-            h1_num += decoded(nqr[d - 1, at], nmr[d - 1, 0:1, 512:640])
-        new = h1v[at, mine] * h1_num / colsum[at]
-        fr[at] = new
+        for p in range(2):
+            at = rows(b, p)
+            h1_num = num[g, at]
+            for d in (3, 1) if p == 0 else (1, 3):
+                send_num(b, d, p).wait_recv()
+                joined = (d == 1) == (p == 0)
+                most = sent_mark(d) + sent_mark(2) if joined else sent_mark(d)
+                h1_num += decoded(nqr[d - 1, at], most)
+            fr[at] = h1v[at, mine] * h1_num / colsum[at]
+        new = fr[256 * b : 256 * b + 256]
         most = most_of(new, 0)
         hq[b, g] = coded(new, most)
         hs[b, g] = jnp.broadcast_to(most, (8, 128))
+        for d in (1, 3):
+            send_h(b, d).start()
         for d in ORDER:
-            for go in send_h(b, d):
-                go.start()
+            send_hs(b, d).start()
+
+    def take_h(b, d):
+        j = at_g(4 - d)
+        value = decoded(hq[b, j], hs[b, j, 0:1])
+        there = pl.ds(pl.multiple_of(j * 128, 128), 128)
+        here = pl.ds(256 * b, 256)
+        h1f[here, there] = value
+        hl[here, there] = value.astype(BF16)
+
+    def take_near(b):
+        for d in (1, 3):
+            send_h(b, d).wait_recv()
+            pass_h(b, d // 3).start()
+        take_h(b, 0)
+        for d in (1, 3):
+            send_hs(b, d).wait_recv()
+            take_h(b, d)
+
+    def take_far(b):
+        send_hs(b, 2).wait_recv()
+        for p in range(2):
+            pass_h(b, p).wait_recv()
+        take_h(b, 2)
+
+    take_near(0)
     fresh = fr[...]
 
     ratio3 = fresh / fit
@@ -252,7 +312,7 @@
     ratio4 = fresh / high(w2, h2_new)
     w2_part = nt(h2_new, ratio4, HI)
     h2_part = jnp.broadcast_to(jnp.sum(h2_new, axis=1, keepdims=True), (64, 128))
-    rows = nt(jnp.ones((8, 128), F32), fresh, HI)
+    h1_rows = nt(jnp.ones((8, 128), F32), fresh, HI)
     for j in range(NG):
         for c in range(NC):
             at = 16 * j + 8 * c
@@ -260,7 +320,7 @@
             sm[c, j, :, 512:640] = h2_part[at : at + 8]
             sm[c, j, :, 640:768] = jnp.zeros((8, 128), F32)
             for k in range(4):
-                sm[c, j, k : k + 1, 640:768] = rows[0:1, k * 128 : (k + 1) * 128]
+                sm[c, j, k : k + 1, 640:768] = h1_rows[0:1, k * 128 : (k + 1) * 128]
 
     sum_c = copy(sm.at[oc], smr, "s0", 0, sibling)
 
@@ -284,21 +344,13 @@
         return copy(h2b.at[g], h2b.at[g], "h2", d - 1, to_g(d))
 
     sum_c.start()
-    for b in range(2):
-        for d in (0,) + ORDER:
-            if d:
-                for go in send_h(b, d):
-                    go.wait_recv()
-            j = at_g(4 - d)
-            value = decoded(hq[b, j], hs[b, j, 0:1])
-            there = pl.ds(pl.multiple_of(j * 128, 128), 128)
-            h1f[block(b), there] = value
-            hl[block(b), there] = value.astype(BF16)
-        if b == 0:
-            sum_c.wait_recv()
-            sv[...] = sm[mc] + smr[...]
-            for d in ORDER:
-                sum_g(d).start()
+    take_near(1)
+    sum_c.wait_recv()
+    sv[...] = sm[mc] + smr[...]
+    for d in ORDER:
+        sum_g(d).start()
+    take_far(0)
+    take_far(1)
 
     def second(h, i):
         d = i + 1
@@ -347,7 +399,7 @@
             for h in range(2):
                 add_up(h, i - 1)
 
-        @pl.when(i == 2)
+        @pl.when(i == 1)
         def _():
             for d in ORDER:
                 sum_g(d).wait_recv()
@@ -356,12 +408,20 @@
             for d in ORDER:
                 send_h2(d).start()
 
-        @pl.when(i == 4)
+        @pl.when(i == 2)
         def _():
             sum_z.wait_recv()
             sx[mx] = sz[...] + szr[...]
             for d in ORDER:
                 sum_x(d).start()
+
+        @pl.when(i == 4)
+        def _():
+            for d in ORDER:
+                sum_x(d).wait_recv()
+            sy[my] = sx[0] + sx[1] + sx[2] + sx[3]
+            for d in ORDER:
+                sum_y(d).start()
 
         return carry
 
@@ -377,46 +437,27 @@
             copy(aps.at[h, d - 1], apr.at[h, d - 1], "qs", k, to),
         )
 
-    for h in range(2):
-        for i in (0, 2, 1):
+    for i in range(3):
+        if i == 1:
+            for d in ORDER:
+                sum_y(d).wait_recv()
+            done = sy[0] + sy[1] + sy[2] + sy[3]
+            sg[mc, g] = done
+            for d in ORDER:
+                all_g(d).start()
+        for h in range(2):
             for go in along(h, i):
                 go.wait_recv()
-        whole = acc[h].reshape(8, 32, 512)
-        for i in range(3):
-            whole += decoded(pqr[h, i].reshape(8, 32, 512), psr[h, i].reshape(8, 1, 512))
-        acc[h] = whole.reshape(4, 2, 32, 512)
-        for d in ORDER:
-            v = acc[h, at_y(d) if h == 0 else at_x(d)]
-            most = most_of(v, 1)
-            aq[h, d - 1] = coded(v, most)
-            aps[h, d - 1] = jnp.broadcast_to(most, (2, 8, 512))
-            for go in across(h, d):
-                go.start()
-    for d in ORDER:
-        sum_x(d).wait_recv()
-    sy[my] = sx[0] + sx[1] + sx[2] + sx[3]
-    for d in ORDER:
-        sum_y(d).start()
-    for d in ORDER:
-        sum_y(d).wait_recv()
-    done = sy[0] + sy[1] + sy[2] + sy[3]
-    sg[mc, g] = done
-    for d in ORDER:
-        all_g(d).start()
-    for h in range(2):
-        for d in ORDER:
-            for go in across(h, d):
-                go.wait_recv()
-        whole = acc[h, my if h == 0 else mx]
-        for k in range(3):
-            whole += decoded(aqr[h, k], apr[h, k, :, 0:1])
-        fin[:, h] = whole
-    most = most_of(fin[oz], 1)
-    lq[...] = coded(fin[oz], most)
-    lps[...] = jnp.broadcast_to(most, (2, 8, 512))
-    last = (copy(lq, lqr, "l", 0, z_pair), copy(lps, lpr, "ls", 0, z_pair))
-    for go in last:
-        go.start()
+            more = decoded(pqr[h, i].reshape(8, 32, 512), psr[h, i].reshape(8, 1, 512))
+            acc[h] += more.reshape(4, 2, 32, 512)
+            if i == 2:
+                for d in ORDER:
+                    v = acc[h, at_y(d) if h == 0 else at_x(d)]
+                    most = most_of(v, 1)
+                    aq[h, d - 1] = coded(v, most)
+                    aps[h, d - 1] = jnp.broadcast_to(most, (2, 8, 512))
+                    for go in across(h, d):
+                        go.start()
     for d in ORDER:
         all_g(d).wait_recv()
     all_c.start()
@@ -429,6 +470,26 @@
     for put in puts:
         put.start()
     rowsum = jnp.concatenate([done[k : k + 1, 640:768] for k in range(4)], axis=1)
+    for h in range(2):
+        whole = acc[h, my if h == 0 else mx]
+        for d in ORDER:
+            for go in across(h, d):
+                go.wait_recv()
+            whole += decoded(aqr[h, d - 1], apr[h, d - 1, :, 0:1])
+        fin[:, h] = whole
+    most = most_of(fin[oz], 1)
+    lq[...] = coded(fin[oz], most)
+    lps[...] = jnp.broadcast_to(most, (2, 8, 512))
+    last = (copy(lq, lqr, "l", 0, z_pair), copy(lps, lpr, "ls", 0, z_pair))
+    for go in last:
+        go.start()
+    all_c.wait_recv()
+    for j in range(NG):
+        for c in range(NC):
+            at = slice(16 * j + 8 * c, 16 * j + 8 * c + 8)
+            w2f[at, :] = w2tv[at, :] * sg[c, j, :, 0:512] / sg[c, j, :, 512:513]
+    puts.append(pltpu.make_async_copy(w2f, w2t_out, loc.at[11]))
+    puts[-1].start()
     for go in last:
         go.wait_recv()
     w1_num = (fin[mz] + decoded(lqr[...], lpr[:, 0:1])).reshape(64, 512)
@@ -436,20 +497,12 @@
     w1f[...] = (w1_now * w1_num / rowsum).astype(BF16)
     puts.append(pltpu.make_async_copy(w1f, w1_out, loc.at[10]))
     puts[-1].start()
-    all_c.wait_recv()
-    for j in range(NG):
-        for c in range(NC):
-            at = slice(16 * j + 8 * c, 16 * j + 8 * c + 8)
-            w2f[at, :] = w2tv[at, :] * sg[c, j, :, 0:512] / sg[c, j, :, 512:513]
-
-    puts.append(pltpu.make_async_copy(w2f, w2t_out, loc.at[11]))
-    puts[-1].start()
 
     for sent in (go_z, sum_c, sum_z, all_c) + last:
         sent.wait_send()
     for d in ORDER:
         for h in range(2):
-            for sent in (near(0, h, d), near(1, h, d), send_num(h, d)) + send_h(h, d):
+            for sent in (near(0, h, d), near(1, h, d), send_hs(h, d)):
                 sent.wait_send()
             for e in ORDER:
                 far(h, e, d).wait_send()
@@ -457,6 +510,12 @@
                 sent.wait_send()
         for sent in (send_marks, send_h2, sum_g, sum_x, sum_y, all_g):
             sent(d).wait_send()
+    for b in range(2):
+        for p in range(2):
+            for sent in (send_diag(b, p), pass_h(b, p), send_h(b, 3 if p else 1)):
+                sent.wait_send()
+            for d in (1, 3):
+                send_num(b, d, p).wait_send()
     for h in range(2):
         for d in range(4):
             forward(h, d).wait_send()
@@ -465,14 +524,18 @@
         put.wait()
 
 
-def finish(*refs):
-    *arrays, sem = refs
-    copies = [
-        pltpu.make_async_copy(arrays[k], arrays[k + 4], sem.at[k]) for k in range(4)
-    ]
-    for go in copies:
+def finish(w1, h1, w2t, h2, w1_out, h1_out, w2t_out, h2_out, w1v, h1v, w2tv, h2v, sem):
+    rows = [pl.ds(128 * k, 128) for k in range(4)]
+    steps = [(h1.at[r], h1v.at[r], h1_out.at[r]) for r in rows]
+    steps += [(w1, w1v, w1_out), (w2t, w2tv, w2t_out), (h2, h2v, h2_out)]
+    loads = [pltpu.make_async_copy(a, v, sem.at[0, k]) for k, (a, v, o) in enumerate(steps)]
+    stores = [pltpu.make_async_copy(v, o, sem.at[1, k]) for k, (a, v, o) in enumerate(steps)]
+    for go in loads:
         go.start()
-    for go in copies:
+    for load, store in zip(loads, stores):
+        load.wait()
+        store.start()
+    for go in stores:
         go.wait()
 
 
@@ -489,7 +552,7 @@
     scratch = [
         (shape, BF16), (shape, jnp.int32), ((512, 512), F32), ((64, 512), F32), ((64, 512), F32),
         ((512, 512), BF16), ((NG, 512, 128), F32), ((3, 512, 128), I16), ((3, 512, 128), I16),
-        ((3, 8, 640), F32), ((3, 8, 640), F32), ((8, 512), F32),
+        ((3, 8, 768), F32), ((3, 8, 768), F32), ((8, 512), F32),
         ((512, 128), F32), ((2, NG, 256, 128), I16), ((2, NG, 8, 128), F32), ((512, 512), F32), ((NG, 64, 128), F32),
         ((2, 4, 4, 2, 2, 32, 512), F32), ((2, 4, 4, 2, 32, 512), F32), ((2, 4, 2, 32, 512), F32),
         ((2, 3, 4, 2, 32, 512), I16), ((2, 3, 4, 2, 32, 512), I16), ((2, 3, 8, 512), F32), ((2, 3, 8, 512), F32),
@@ -519,7 +582,8 @@
         out_shape=outs,
         in_specs=[anywhere] * 4,
         out_specs=(anywhere,) * 4,
-        scratch_shapes=[pltpu.SemaphoreType.DMA((4,))],
+        scratch_shapes=[pltpu.VMEM(o.shape, o.dtype) for o in outs]
+        + [pltpu.SemaphoreType.DMA((2, 7))],
     )(*moved)
     return w1_new, h1_new, w2t_new.T, h2_new
 

time: 141 us -> 96 us (0.68); the launches traced: 141 us -> 94.4 us
  Pallas kernels: 140 us -> 93.7 us
    pallas_call x1, Pallas kernels: 42.8 us -> 2.14 us  [on_device(): pl.pallas_call(finish, out_shape=outs, in_specs=[anywhere] * 4, out_specs...]
    pallas_call x1, Pallas kernels: 97.3 us -> 91.6 us  [on_device(): pl.pallas_call(kernel, out_shape=outs, in_specs=[anywhere] * 5, out_specs...]
where the time goes in v4:
time: 96 us; the launch traced here: 94.4 us
  Pallas kernels  93.7 us (98%)
    pallas_call x1, Pallas kernels, on_device(): pl.pallas_call(kernel, out_shape=outs, in_specs=[anywhere] * 5, out_specs...  91.6 us
    pallas_call x1, Pallas kernels, on_device(): pl.pallas_call(finish, out_shape=outs, in_specs=[anywhere] * 4, out_specs...  2.14 us

profile of v4, /device:TPU:1, one launch (start us, length us, event | category | flops | bytes accessed | tf_op | source)
XLA Modules:
  0.0 94.4 jit_solution(4744475600377749801)
XLA Ops:
  0.6 91.6 %shard_map.84 = (bf16[64,512]{1,0:T(8,128)(2,1)}, f32[512,512]{1,0:T(8,128)}, f32[64,512]{1,0:T(8,128)}, f32[64,512]{1,0:T(8,128)}) custom-call(s32[4,4,2,2,2,32,512]{6,5,4,3,2,1,0:T(8,128)} %bitcast.4, bf16[2,32,512]{2,1,0:T(8,128)(2,1)} %bitcast.6, f32[512,512]{1,0:T(8,128)} %h1.1, f32[64,512]{1,0:T(8,128)} %bitcast.5, f32[64,512]{1,0:T(8,128)} %h2.1), custom_call_target="tpu_custom_call" | custom-call | tf_op jit(solution)/shard_map/pallas_call | solution.py:565
  92.2 2.1 %shard_map.85 = (bf16[64,512]{1,0:T(8,128)(2,1)}, f32[512,512]{1,0:T(8,128)}, f32[64,512]{1,0:T(8,128)}, f32[64,512]{1,0:T(8,128)}) custom-call(bf16[64,512]{1,0:T(8,128)(2,1)} %get-tuple-element.12.w1, f32[512,512]{1,0:T(8,128)} %get-tuple-element.13.h1, f32[64,512]{1,0:T(8,128)} %get-tuple-element.14.w2t, f32[64,512]{1,0:T(8,128)} %get-tuple-element.15.h2), custom_call_target="tpu_custom_call" | custom-call | tf_op jit(solution)/shard_map/pallas_call | solution.py:580

commit v5 on v4

--- a/solution.py
+++ b/solution.py
@@ -13,8 +13,8 @@
 ORDER = (1, 3, 2)
 
 SIZES = dict(
-    z=1, a2=12, a3=18, f=8, m=3, nd=4, n=8, hb=4, hf=4, hs=6, h2=3, e1=8, p=6, ps=6, q=6, qs=6, l=1, ls=1,
-    s0=1, s1=3, s2=1, s3=3, s4=3, s5=3, s6=1,
+    z=1, a2=12, a3=36, f=8, m=3, nd=4, n=8, hb=4, hf=4, hs=6, h2=3, e1=8, p=6, ps=6, q=6, qs=6, l=1, ls=1,
+    s0=1, s1=3, s2=3, s3=1, s4=3, s5=3, s6=1,
 )
 PLACE, S_ALL = {}, 0
 for _name, _size in SIZES.items():
@@ -47,9 +47,9 @@
 def kernel(
     counts, w1, h1, w2t, h2,
     w1_out, h1_out, w2t_out, h2_out,
-    wg, cnt, h1v, w2tv, h2v, hl, num, nq, nqr, nm, nmr, cs, fr, hq, hs, h1f, h2b,
+    wg, cnt, h1v, w2tv, h2v, hl, num, nq, nqr, nm, nmr, cs, fr, hq, hs, h2b,
     rb, e1r, acc, pq, pqr, ps, psr, aq, aqr, aps, apr, fin, lq, lqr, lps, lpr,
-    sm, smr, sv, svr, sz, szr, sx, sy, sg, w1f, w2f,
+    sm, smr, sv, svr, sz, szr, sx, sy, sg,
     snd, rcv, loc,
 ):
     g = lax.axis_index("gene")
@@ -131,20 +131,26 @@
     def column(h, d):
         return wg.at[:, at_y(4 - d), :, mc, 0] if h == 0 else wg.at[at_x(4 - d), :, :, mc, 1]
 
-    def far(h, e, d):
-        src = wg.at[mx, at_y(4 - e), :, mc, 1] if h else wg.at[at_x(4 - e), my, :, mc, 0]
-        return copy(src, src, "a3", 9 * h + 3 * (e - 1) + d - 1, to_x(d) if h else to_y(d))
+    def far(k, h, e, d):
+        z = oz if k else mz
+        src = wg.at[mx, at_y(4 - e), z, mc, 1] if h else wg.at[at_x(4 - e), my, z, mc, 0]
+        to = to_x(d) if h else to_y(d)
+        return copy(src, src, "a3", 18 * k + 9 * h + 3 * (e - 1) + d - 1, to)
 
     def forward(h, d):
         src = column(h, d)
         return copy(src, src, "f", 4 * h + d, sibling)
 
-    for e in ORDER:
-        for h in range(2):
-            near(0, h, e).wait_recv()
-            near(1, h, e).wait_recv()
-            for d in ORDER:
-                far(h, e, d).start()
+    for k in range(2):
+        for e in ORDER:
+            for h in range(2):
+                near(k, h, e).wait_recv()
+                for d in (1, 3):
+                    far(k, h, e, d).start()
+    for k in range(2):
+        for e in ORDER:
+            for h in range(2):
+                far(k, h, e, 2).start()
     for h in range(2):
         forward(h, 0).start()
 
@@ -153,7 +159,8 @@
     def pass_on(d):
         for h in range(2):
             for e in ORDER:
-                far(h, e, d).wait_recv()
+                far(0, h, e, d).wait_recv()
+                far(1, h, e, d).wait_recv()
             forward(h, d).start()
 
     def first(w, v):
@@ -237,13 +244,25 @@
     def sent_mark(d, k=0):
         return nmr[d - 1, 0:1, 512 + 128 * k : 640 + 128 * k]
 
-    for b in range(2):
+    def start_diag(b):
         for p in range(2):
             code_num(b, 2, p, None, far_most)
             send_diag(b, p).start()
+
+    def start_own(b):
         for d, p in ((1, 1), (3, 0)):
             code_num(b, d, p, None, mark(d))
             send_num(b, d, p).start()
+
+    def start_joined(b):
+        for d, p in ((1, 0), (3, 1)):
+            send_diag(b, p).wait_recv()
+            code_num(b, d, p, sent_mark(d, 1), mark(d) + sent_mark(d, 1))
+            send_num(b, d, p).start()
+
+    start_diag(0)
+    start_own(0)
+    start_diag(1)
     read_w2.wait()
     read_h2.wait()
     w2 = jnp.transpose(w2tv[...])
@@ -252,11 +271,9 @@
     fit = high(w2, h2_mine)
     for d in ORDER:
         send_marks(d).wait_recv()
-    for b in range(2):
-        for d, p in ((1, 0), (3, 1)):
-            send_diag(b, p).wait_recv()
-            code_num(b, d, p, sent_mark(d, 1), mark(d) + sent_mark(d, 1))
-            send_num(b, d, p).start()
+    start_joined(0)
+    start_own(1)
+    start_joined(1)
     parts = cs[...] + nmr[0, :, 0:512] + nmr[1, :, 0:512] + nmr[2, :, 0:512]
     total = jnp.sum(parts, axis=0, keepdims=True)
     colsum = jnp.transpose(jnp.broadcast_to(total, (128, 512)))
@@ -284,7 +301,7 @@
         value = decoded(hq[b, j], hs[b, j, 0:1])
         there = pl.ds(pl.multiple_of(j * 128, 128), 128)
         here = pl.ds(256 * b, 256)
-        h1f[here, there] = value
+        h1_out[here, there] = value
         hl[here, there] = value.astype(BF16)
 
     def take_near(b):
@@ -302,7 +319,6 @@
             pass_h(b, p).wait_recv()
         take_h(b, 2)
 
-    take_near(0)
     fresh = fr[...]
 
     ratio3 = fresh / fit
@@ -324,19 +340,19 @@
 
     sum_c = copy(sm.at[oc], smr, "s0", 0, sibling)
 
+    def sum_x(d):
+        return copy(sv.at[at_x(d)], svr.at[d - 1], "s1", d - 1, to_x(d))
+
+    def sum_y(d):
+        return copy(sy.at[my], sy.at[my], "s2", d - 1, to_y(d))
+
+    sum_z = copy(sz, szr, "s3", 0, z_pair)
+
     def sum_g(d):
-        return copy(sv.at[at_g(d)], svr.at[d - 1], "s1", d - 1, to_g(d))
-
-    sum_z = copy(sz, szr, "s2", 0, z_pair)
-
-    def sum_x(d):
-        return copy(sx.at[mx], sx.at[mx], "s3", d - 1, to_x(d))
-
-    def sum_y(d):
-        return copy(sy.at[my], sy.at[my], "s4", d - 1, to_y(d))
-
-    def all_g(d):
-        return copy(sg.at[mc, g], sg.at[mc, g], "s5", d - 1, to_g(d))
+        return copy(sx.at[g], sx.at[g], "s4", d - 1, to_g(d))
+
+    def all_x(d):
+        return copy(sg.at[mc, mx], sg.at[mc, mx], "s5", d - 1, to_x(d))
 
     all_c = copy(sg.at[mc], sg.at[mc], "s6", 0, sibling)
 
@@ -344,16 +360,29 @@
         return copy(h2b.at[g], h2b.at[g], "h2", d - 1, to_g(d))
 
     sum_c.start()
-    take_near(1)
+    take_near(0)
     sum_c.wait_recv()
     sv[...] = sm[mc] + smr[...]
     for d in ORDER:
-        sum_g(d).start()
+        sum_x(d).start()
+    take_near(1)
+    for d in ORDER:
+        sum_x(d).wait_recv()
+    sy[my] = sv[mx] + svr[0] + svr[1] + svr[2]
+    for d in ORDER:
+        sum_y(d).start()
     take_far(0)
     take_far(1)
+    for d in ORDER:
+        sum_y(d).wait_recv()
+    sz[...] = sy[0] + sy[1] + sy[2] + sy[3]
+    sum_z.start()
+
+    def place(i):
+        return (i + 2 + i // 2 + 2 * (i // 3)) % 4
 
     def second(h, i):
-        d = i + 1
+        d = place(i)
         w = wg[:, at_y(d), :, :, 1] if h else wg[at_x(d), :, :, :, 0]
         v = cnt[:, at_y(d), :, :, 1] if h else cnt[at_x(d), :, :, :, 0]
         approx = jnp.dot(w.reshape(512, 512), hl[...], preferred_element_type=F32)
@@ -364,7 +393,7 @@
         return copy(rb.at[h, i, :, :, oc], e1r.at[h, i], "e1", 4 * h + i, sibling)
 
     def along(h, i):
-        to = to_x(i + 1) if h == 0 else to_y(i + 1)
+        to = to_x(place(i)) if h == 0 else to_y(place(i))
         return (
             copy(pq.at[h, i], pqr.at[h, i], "p", 3 * h + i, to),
             copy(ps.at[h, i], psr.at[h, i], "ps", 3 * h + i, to),
@@ -388,46 +417,37 @@
             acc[h] = both
 
     def second_step(i, carry):
-        @pl.when(i < 4)
-        def _():
-            for h in range(2):
+        for h in range(2):
+
+            @pl.when(i < 4)
+            def _():
                 second(h, i)
                 to_sibling(h, i).start()
 
-        @pl.when(i > 0)
+            @pl.when(i > 0)
+            def _():
+                add_up(h, i - 1)
+
+        @pl.when(i == 1)
         def _():
-            for h in range(2):
-                add_up(h, i - 1)
-
-        @pl.when(i == 1)
+            sum_z.wait_recv()
+            sx[g] = sz[...] + szr[...]
+            for d in ORDER:
+                sum_g(d).start()
+            for d in ORDER:
+                send_h2(d).start()
+
+        @pl.when(i == 3)
         def _():
             for d in ORDER:
                 sum_g(d).wait_recv()
-            sz[...] = sv[g] + svr[0] + svr[1] + svr[2]
-            sum_z.start()
+            sg[mc, mx] = sx[0] + sx[1] + sx[2] + sx[3]
             for d in ORDER:
-                send_h2(d).start()
-
-        @pl.when(i == 2)
-        def _():
-            sum_z.wait_recv()
-            sx[mx] = sz[...] + szr[...]
-            for d in ORDER:
-                sum_x(d).start()
-
-        @pl.when(i == 4)
-        def _():
-            for d in ORDER:
-                sum_x(d).wait_recv()
-            sy[my] = sx[0] + sx[1] + sx[2] + sx[3]
-            for d in ORDER:
-                sum_y(d).start()
+                all_x(d).start()
 
         return carry
 
     lax.fori_loop(0, 5, second_step, 0)
-    put_h1 = pltpu.make_async_copy(h1f, h1_out, loc.at[5])
-    put_h1.start()
 
     def across(h, d):
         to = to_y(d) if h == 0 else to_x(d)
@@ -438,13 +458,6 @@
         )
 
     for i in range(3):
-        if i == 1:
-            for d in ORDER:
-                sum_y(d).wait_recv()
-            done = sy[0] + sy[1] + sy[2] + sy[3]
-            sg[mc, g] = done
-            for d in ORDER:
-                all_g(d).start()
         for h in range(2):
             for go in along(h, i):
                 go.wait_recv()
@@ -459,17 +472,13 @@
                     for go in across(h, d):
                         go.start()
     for d in ORDER:
-        all_g(d).wait_recv()
+        all_x(d).wait_recv()
     all_c.start()
     for d in ORDER:
         send_h2(d).wait_recv()
-    puts = [
-        pltpu.make_async_copy(h2b.at[j], h2_out.at[:, 128 * j : 128 * j + 128], loc.at[6 + j])
-        for j in range(NG)
-    ]
-    for put in puts:
-        put.start()
-    rowsum = jnp.concatenate([done[k : k + 1, 640:768] for k in range(4)], axis=1)
+    for j in range(NG):
+        h2_out[:, 128 * j : 128 * j + 128] = h2b[j]
+    rowsum = jnp.concatenate([sg[mc, mx, k : k + 1, 640:768] for k in range(4)], axis=1)
     for h in range(2):
         whole = acc[h, my if h == 0 else mx]
         for d in ORDER:
@@ -487,16 +496,12 @@
     for j in range(NG):
         for c in range(NC):
             at = slice(16 * j + 8 * c, 16 * j + 8 * c + 8)
-            w2f[at, :] = w2tv[at, :] * sg[c, j, :, 0:512] / sg[c, j, :, 512:513]
-    puts.append(pltpu.make_async_copy(w2f, w2t_out, loc.at[11]))
-    puts[-1].start()
+            w2t_out[at, :] = w2tv[at, :] * sg[c, j, :, 0:512] / sg[c, j, :, 512:513]
     for go in last:
         go.wait_recv()
     w1_num = (fin[mz] + decoded(lqr[...], lpr[:, 0:1])).reshape(64, 512)
     w1_now = wg[mx, my, mz, mc].astype(F32).reshape(64, 512)
-    w1f[...] = (w1_now * w1_num / rowsum).astype(BF16)
-    puts.append(pltpu.make_async_copy(w1f, w1_out, loc.at[10]))
-    puts[-1].start()
+    w1_out[...] = (w1_now * w1_num / rowsum).astype(BF16)
 
     for sent in (go_z, sum_c, sum_z, all_c) + last:
         sent.wait_send()
@@ -505,10 +510,11 @@
             for sent in (near(0, h, d), near(1, h, d), send_hs(h, d)):
                 sent.wait_send()
             for e in ORDER:
-                far(h, e, d).wait_send()
+                far(0, h, e, d).wait_send()
+                far(1, h, e, d).wait_send()
             for sent in along(h, d - 1) + across(h, d):
                 sent.wait_send()
-        for sent in (send_marks, send_h2, sum_g, sum_x, sum_y, all_g):
+        for sent in (send_marks, send_h2, sum_g, sum_x, sum_y, all_x):
             sent(d).wait_send()
     for b in range(2):
         for p in range(2):
@@ -520,27 +526,20 @@
         for d in range(4):
             forward(h, d).wait_send()
             to_sibling(h, d).wait_send()
-    for put in puts + [put_h1]:
-        put.wait()
-
-
-def finish(w1, h1, w2t, h2, w1_out, h1_out, w2t_out, h2_out, w1v, h1v, w2tv, h2v, sem):
-    rows = [pl.ds(128 * k, 128) for k in range(4)]
-    steps = [(h1.at[r], h1v.at[r], h1_out.at[r]) for r in rows]
-    steps += [(w1, w1v, w1_out), (w2t, w2tv, w2t_out), (h2, h2v, h2_out)]
-    loads = [pltpu.make_async_copy(a, v, sem.at[0, k]) for k, (a, v, o) in enumerate(steps)]
-    stores = [pltpu.make_async_copy(v, o, sem.at[1, k]) for k, (a, v, o) in enumerate(steps)]
-    for go in loads:
+
+
+def finish(w1, h1, w2t, h2, w1_out, h1_out, w2t_out, h2_out, sem):
+    pairs = ((h1, h1_out), (w1, w1_out), (w2t, w2t_out), (h2, h2_out))
+    stores = [pltpu.make_async_copy(a, b, sem.at[k]) for k, (a, b) in enumerate(pairs)]
+    for go in stores:
         go.start()
-    for load, store in zip(loads, stores):
-        load.wait()
-        store.start()
     for go in stores:
         go.wait()
 
 
 def on_device(counts, w1, h1, w2, h2):
     anywhere = pl.BlockSpec(memory_space=pl.ANY)
+    vmem = pl.BlockSpec(memory_space=pltpu.VMEM)
     shape = (NX, NY, NZ, NC, 2, 32, 512)
     sds = jax.ShapeDtypeStruct
     outs = (
@@ -553,25 +552,24 @@
         (shape, BF16), (shape, jnp.int32), ((512, 512), F32), ((64, 512), F32), ((64, 512), F32),
         ((512, 512), BF16), ((NG, 512, 128), F32), ((3, 512, 128), I16), ((3, 512, 128), I16),
         ((3, 8, 768), F32), ((3, 8, 768), F32), ((8, 512), F32),
-        ((512, 128), F32), ((2, NG, 256, 128), I16), ((2, NG, 8, 128), F32), ((512, 512), F32), ((NG, 64, 128), F32),
+        ((512, 128), F32), ((2, NG, 256, 128), I16), ((2, NG, 8, 128), F32), ((NG, 64, 128), F32),
         ((2, 4, 4, 2, 2, 32, 512), F32), ((2, 4, 4, 2, 32, 512), F32), ((2, 4, 2, 32, 512), F32),
         ((2, 3, 4, 2, 32, 512), I16), ((2, 3, 4, 2, 32, 512), I16), ((2, 3, 8, 512), F32), ((2, 3, 8, 512), F32),
         ((2, 3, 2, 32, 512), I16), ((2, 3, 2, 32, 512), I16), ((2, 3, 2, 8, 512), F32), ((2, 3, 2, 8, 512), F32),
         ((2, 2, 32, 512), F32), ((2, 32, 512), I16), ((2, 32, 512), I16), ((2, 8, 512), F32), ((2, 8, 512), F32),
         ((2, NG, 8, 768), F32), ((NG, 8, 768), F32), ((NG, 8, 768), F32), ((3, 8, 768), F32), ((8, 768), F32),
         ((8, 768), F32), ((4, 8, 768), F32), ((4, 8, 768), F32), ((2, NG, 8, 768), F32),
-        ((64, 512), BF16), ((64, 512), F32),
     ]
     moved = pl.pallas_call(
         kernel,
-        out_shape=outs,
+        out_shape=tuple(pltpu.VMEM(o.shape, o.dtype) for o in outs),
         in_specs=[anywhere] * 5,
-        out_specs=(anywhere,) * 4,
+        out_specs=(vmem,) * 4,
         scratch_shapes=[pltpu.VMEM(*s) for s in scratch]
         + [
             pltpu.SemaphoreType.DMA((S_ALL,)),
             pltpu.SemaphoreType.DMA((S_ALL,)),
-            pltpu.SemaphoreType.DMA((12,)),
+            pltpu.SemaphoreType.DMA((5,)),
         ],
         compiler_params=pltpu.CompilerParams(
             collective_id=0, has_side_effects=True, vmem_limit_bytes=56 * 1024 * 1024
@@ -580,11 +578,10 @@
     w1_new, h1_new, w2t_new, h2_new = pl.pallas_call(
         finish,
         out_shape=outs,
-        in_specs=[anywhere] * 4,
+        in_specs=[vmem] * 4,
         out_specs=(anywhere,) * 4,
-        scratch_shapes=[pltpu.VMEM(o.shape, o.dtype) for o in outs]
-        + [pltpu.SemaphoreType.DMA((2, 7))],
-    )(*moved)
+        scratch_shapes=[pltpu.SemaphoreType.DMA((4,))],
+    )(*[pltpu.with_memory_space_constraint(m, pltpu.VMEM) for m in moved])
     return w1_new, h1_new, w2t_new.T, h2_new
 
 

time: 96 us -> 90.9 us (0.947); the launches traced: 94.4 us -> 90.8 us
  Pallas kernels: 93.7 us -> 90.2 us
    pallas_call x2, Pallas kernels: 93.7 us -> 90.2 us  [the longest x1 89.1 us: on_device(): pl.pallas_call(kernel, out_shape=tuple((pltpu.VMEM(o.shape, o.dtype) for...]
where the time goes in v5:
time: 90.9 us; the launch traced here: 90.8 us
  Pallas kernels  90.2 us (99%)
    pallas_call x1, Pallas kernels, on_device(): pl.pallas_call(kernel, out_shape=tuple((pltpu.VMEM(o.shape, o.dtype) for...  89.1 us

profile of v5, /device:TPU:1, one launch (start us, length us, event | category | flops | bytes accessed | tf_op | source)
XLA Modules:
  0.0 90.8 jit_solution(16778147012363519681)
XLA Ops:
  0.6 89.1 %shard_map.84 = (bf16[64,512]{1,0:T(8,128)(2,1)S(1)}, f32[512,512]{1,0:T(8,128)S(1)}, f32[64,512]{1,0:T(8,128)S(1)}, f32[64,512]{1,0:T(8,128)S(1)}) custom-call(s32[4,4,2,2,2,32,512]{6,5,4,3,2,1,0:T(8,128)} %bitcast.4, bf16[2,32,512]{2,1,0:T(8,128)(2,1)} %bitcast.6, f32[512,512]{1,0:T(8,128)} %h1.1, f32[64,512]{1,0:T(8,128)} %bitcast.5, f32[64,512]{1,0:T(8,128)} %h2.1), custom_call_target="tpu_custom_call" | custom-call | tf_op jit(solution)/shard_map/pallas_call | solution.py:563
  89.7 1.1 %shard_map.85 = (bf16[64,512]{1,0:T(8,128)(2,1)}, f32[512,512]{1,0:T(8,128)}, f32[64,512]{1,0:T(8,128)}, f32[64,512]{1,0:T(8,128)}) custom-call(bf16[64,512]{1,0:T(8,128)(2,1)S(1)} %get-tuple-element.12.w1, f32[512,512]{1,0:T(8,128)S(1)} %get-tuple-element.13.h1, f32[64,512]{1,0:T(8,128)S(1)} %get-tuple-element.14.w2t, f32[64,512]{1,0:T(8,128)S(1)} %get-tuple-element.15.h2), custom_call_target="tpu_custom_call" | custom-call | tf_op jit(solution)/shard_map/pallas_call | solution.py:578

commit v6 on v5

--- a/solution.py
+++ b/solution.py
@@ -13,7 +13,7 @@
 ORDER = (1, 3, 2)
 
 SIZES = dict(
-    z=1, a2=12, a3=36, f=8, m=3, nd=4, n=8, hb=4, hf=4, hs=6, h2=3, e1=8, p=6, ps=6, q=6, qs=6, l=1, ls=1,
+    z=1, a2=12, a3=36, f=8, m=3, nd=4, n=8, hb=4, hf=4, hs=6, h2=3, e1=8, pd=4, pds=4, p=8, ps=4, q=6, qs=6, l=1, ls=1,
     s0=1, s1=3, s2=3, s3=1, s4=3, s5=3, s6=1,
 )
 PLACE, S_ALL = {}, 0
@@ -40,6 +40,18 @@
     return jnp.round(v * (TOP / most)).astype(jnp.int32).astype(I16)
 
 
+def coded_by_8(v):
+    rows = v.reshape(8, 8, 512)
+    most = most_of(rows, 1)
+    whole = jnp.round(rows * (TOP / most)).astype(jnp.int32)
+    return whole.reshape(v.shape).astype(I16), most.reshape(8, 512)
+
+
+def decoded_by_8(q, most):
+    whole = q.astype(jnp.int32).astype(F32).reshape(8, 8, 512)
+    return (whole * (most.reshape(8, 1, 512) * (1.0 / TOP))).reshape(q.shape)
+
+
 def decoded(q, most):
     return q.astype(jnp.int32).astype(F32) * (most * (1.0 / TOP))
 
@@ -48,7 +60,7 @@
     counts, w1, h1, w2t, h2,
     w1_out, h1_out, w2t_out, h2_out,
     wg, cnt, h1v, w2tv, h2v, hl, num, nq, nqr, nm, nmr, cs, fr, hq, hs, h2b,
-    rb, e1r, acc, pq, pqr, ps, psr, aq, aqr, aps, apr, fin, lq, lqr, lps, lpr,
+    rb, e1r, acc, pq, pqr, ps, psr, psd, held, aq, aqr, aps, apr, fin, lq, lqr, lps, lpr,
     sm, smr, sv, svr, sz, szr, sx, sy, sg,
     snd, rcv, loc,
 ):
@@ -373,10 +385,6 @@
         sum_y(d).start()
     take_far(0)
     take_far(1)
-    for d in ORDER:
-        sum_y(d).wait_recv()
-    sz[...] = sy[0] + sy[1] + sy[2] + sy[3]
-    sum_z.start()
 
     def place(i):
         return (i + 2 + i // 2 + 2 * (i // 3)) % 4
@@ -392,29 +400,65 @@
     def to_sibling(h, i):
         return copy(rb.at[h, i, :, :, oc], e1r.at[h, i], "e1", 4 * h + i, sibling)
 
-    def along(h, i):
-        to = to_x(place(i)) if h == 0 else to_y(place(i))
+    def to(h, d):
+        return to_y(d) if h else to_x(d)
+
+    def half(p):
+        return slice(2 * p, 2 * p + 2)
+
+    def two_on(h, p):
+        d, k = 3 if p else 1, 2 * h + p
         return (
-            copy(pq.at[h, i], pqr.at[h, i], "p", 3 * h + i, to),
-            copy(ps.at[h, i], psr.at[h, i], "ps", 3 * h + i, to),
+            copy(pq.at[h, 0, half(p)], pqr.at[h, 0, half(p)], "pd", k, to(h, d)),
+            copy(ps.at[h, 0], psd.at[h, p], "pds", k, to(h, d)),
         )
+
+    def direct(h, i, p):
+        k = 4 * h + 2 * (i - 1) + p
+        return copy(pq.at[h, i, half(p)], pqr.at[h, i, half(p)], "p", k, to(h, place(i)))
+
+    def steps(h, i):
+        return copy(ps.at[h, i], psr.at[h, i], "ps", 2 * h + i - 1, to(h, place(i)))
+
+    def code_half(h, i, p, v):
+        most = most_of(v, 1)
+        pq[h, i, half(p)] = coded(v, most).reshape(2, 2, 32, 512)
+        ps[h, i, 4 * p : 4 * p + 4] = most.reshape(4, 512)
+        direct(h, i, p).start()
 
     def add_up(h, i):
         to_sibling(h, i).wait_recv()
         both = rb[h, i, :, :, mc] + e1r[h, i]
 
-        @pl.when(i < 3)
+        @pl.when(i == 0)
         def _():
             v = both.reshape(8, 32, 512)
             most = most_of(v, 1)
-            pq[h, i] = coded(v, most).reshape(4, 2, 32, 512)
-            ps[h, i] = most.reshape(8, 512)
-            for go in along(h, i):
-                go.start()
+            pq[h, 0] = coded(v, most).reshape(4, 2, 32, 512)
+            ps[h, 0] = most.reshape(8, 512)
+            for p in range(2):
+                for go in two_on(h, p):
+                    go.start()
+
+        for k in (1, 2):
+
+            @pl.when(i == k)
+            def _():
+                code_half(h, k, k - 1, both[half(k - 1)].reshape(4, 32, 512))
+                held[h, k - 1] = both[half(2 - k)]
 
         @pl.when(i == 3)
         def _():
             acc[h] = both
+
+    def join(h, i):
+        p = 2 - i
+        for go in two_on(h, p):
+            go.wait_recv()
+        q = pqr[h, 0, half(p)].reshape(4, 32, 512)
+        more = decoded(q, psd[h, p, 4 * p : 4 * p + 4].reshape(4, 1, 512))
+        code_half(h, i, p, held[h, i - 1].reshape(4, 32, 512) + more)
+        steps(h, i).start()
 
     def second_step(i, carry):
         for h in range(2):
@@ -429,21 +473,20 @@
                 add_up(h, i - 1)
 
         @pl.when(i == 1)
+        def _():
+            for d in ORDER:
+                sum_y(d).wait_recv()
+            sz[...] = sy[0] + sy[1] + sy[2] + sy[3]
+            sum_z.start()
+            for d in ORDER:
+                send_h2(d).start()
+
+        @pl.when(i == 3)
         def _():
             sum_z.wait_recv()
             sx[g] = sz[...] + szr[...]
             for d in ORDER:
                 sum_g(d).start()
-            for d in ORDER:
-                send_h2(d).start()
-
-        @pl.when(i == 3)
-        def _():
-            for d in ORDER:
-                sum_g(d).wait_recv()
-            sg[mc, mx] = sx[0] + sx[1] + sx[2] + sx[3]
-            for d in ORDER:
-                all_x(d).start()
 
         return carry
 
@@ -457,18 +500,25 @@
             copy(aps.at[h, d - 1], apr.at[h, d - 1], "qs", k, to),
         )
 
-    for i in range(3):
-        for h in range(2):
-            for go in along(h, i):
-                go.wait_recv()
+    for h in range(2):
+        for i in (1, 2):
+            join(h, i)
+    for d in ORDER:
+        sum_g(d).wait_recv()
+    sg[mc, mx] = sx[0] + sx[1] + sx[2] + sx[3]
+    for d in ORDER:
+        all_x(d).start()
+    for h in range(2):
+        for i in (1, 2):
+            for p in range(2):
+                direct(h, i, p).wait_recv()
+            steps(h, i).wait_recv()
             more = decoded(pqr[h, i].reshape(8, 32, 512), psr[h, i].reshape(8, 1, 512))
             acc[h] += more.reshape(4, 2, 32, 512)
             if i == 2:
                 for d in ORDER:
                     v = acc[h, at_y(d) if h == 0 else at_x(d)]
-                    most = most_of(v, 1)
-                    aq[h, d - 1] = coded(v, most)
-                    aps[h, d - 1] = jnp.broadcast_to(most, (2, 8, 512))
+                    aq[h, d - 1], aps[h, d - 1] = coded_by_8(v)
                     for go in across(h, d):
                         go.start()
     for d in ORDER:
@@ -484,11 +534,9 @@
         for d in ORDER:
             for go in across(h, d):
                 go.wait_recv()
-            whole += decoded(aqr[h, d - 1], apr[h, d - 1, :, 0:1])
+            whole += decoded_by_8(aqr[h, d - 1], apr[h, d - 1])
         fin[:, h] = whole
-    most = most_of(fin[oz], 1)
-    lq[...] = coded(fin[oz], most)
-    lps[...] = jnp.broadcast_to(most, (2, 8, 512))
+    lq[...], lps[...] = coded_by_8(fin[oz])
     last = (copy(lq, lqr, "l", 0, z_pair), copy(lps, lpr, "ls", 0, z_pair))
     for go in last:
         go.start()
@@ -499,7 +547,7 @@
             w2t_out[at, :] = w2tv[at, :] * sg[c, j, :, 0:512] / sg[c, j, :, 512:513]
     for go in last:
         go.wait_recv()
-    w1_num = (fin[mz] + decoded(lqr[...], lpr[:, 0:1])).reshape(64, 512)
+    w1_num = (fin[mz] + decoded_by_8(lqr[...], lpr[...])).reshape(64, 512)
     w1_now = wg[mx, my, mz, mc].astype(F32).reshape(64, 512)
     w1_out[...] = (w1_now * w1_num / rowsum).astype(BF16)
 
@@ -512,7 +560,7 @@
             for e in ORDER:
                 far(0, h, e, d).wait_send()
                 far(1, h, e, d).wait_send()
-            for sent in along(h, d - 1) + across(h, d):
+            for sent in across(h, d):
                 sent.wait_send()
         for sent in (send_marks, send_h2, sum_g, sum_x, sum_y, all_x):
             sent(d).wait_send()
@@ -523,6 +571,9 @@
             for d in (1, 3):
                 send_num(b, d, p).wait_send()
     for h in range(2):
+        for p in range(2):
+            for sent in two_on(h, p) + (direct(h, 1, p), direct(h, 2, p), steps(h, 1 + p)):
+                sent.wait_send()
         for d in range(4):
             forward(h, d).wait_send()
             to_sibling(h, d).wait_send()
@@ -555,8 +606,9 @@
         ((512, 128), F32), ((2, NG, 256, 128), I16), ((2, NG, 8, 128), F32), ((NG, 64, 128), F32),
         ((2, 4, 4, 2, 2, 32, 512), F32), ((2, 4, 4, 2, 32, 512), F32), ((2, 4, 2, 32, 512), F32),
         ((2, 3, 4, 2, 32, 512), I16), ((2, 3, 4, 2, 32, 512), I16), ((2, 3, 8, 512), F32), ((2, 3, 8, 512), F32),
-        ((2, 3, 2, 32, 512), I16), ((2, 3, 2, 32, 512), I16), ((2, 3, 2, 8, 512), F32), ((2, 3, 2, 8, 512), F32),
-        ((2, 2, 32, 512), F32), ((2, 32, 512), I16), ((2, 32, 512), I16), ((2, 8, 512), F32), ((2, 8, 512), F32),
+        ((2, 2, 8, 512), F32), ((2, 2, 2, 2, 32, 512), F32),
+        ((2, 3, 2, 32, 512), I16), ((2, 3, 2, 32, 512), I16), ((2, 3, 8, 512), F32), ((2, 3, 8, 512), F32),
+        ((2, 2, 32, 512), F32), ((2, 32, 512), I16), ((2, 32, 512), I16), ((8, 512), F32), ((8, 512), F32),
         ((2, NG, 8, 768), F32), ((NG, 8, 768), F32), ((NG, 8, 768), F32), ((3, 8, 768), F32), ((8, 768), F32),
         ((8, 768), F32), ((4, 8, 768), F32), ((4, 8, 768), F32), ((2, NG, 8, 768), F32),
     ]

time: 90.9 us -> 85.4 us (0.939)
  Pallas kernels: 90.2 us -> 84.4 us
    pallas_call x1, Pallas kernels: 89.1 us -> 83.3 us  [on_device(): pl.pallas_call(kernel, out_shape=tuple((pltpu.VMEM(o.shape, o.dtype) for...]
where the time goes in v6:
time: 85.4 us; the launch traced here: 85 us
  Pallas kernels  84.4 us (99%)
    pallas_call x1, Pallas kernels, on_device(): pl.pallas_call(kernel, out_shape=tuple((pltpu.VMEM(o.shape, o.dtype) for...  83.3 us

profile of v6, /device:TPU:1, one launch (start us, length us, event | category | flops | bytes accessed | tf_op | source)
XLA Modules:
  0.0 85.0 jit_solution(9863904414551160903)
XLA Ops:
  0.6 83.3 %shard_map.84 = (bf16[64,512]{1,0:T(8,128)(2,1)S(1)}, f32[512,512]{1,0:T(8,128)S(1)}, f32[64,512]{1,0:T(8,128)S(1)}, f32[64,512]{1,0:T(8,128)S(1)}) custom-call(s32[4,4,2,2,2,32,512]{6,5,4,3,2,1,0:T(8,128)} %bitcast.4, bf16[2,32,512]{2,1,0:T(8,128)(2,1)} %bitcast.6, f32[512,512]{1,0:T(8,128)} %h1.1, f32[64,512]{1,0:T(8,128)} %bitcast.5, f32[64,512]{1,0:T(8,128)} %h2.1), custom_call_target="tpu_custom_call" | custom-call | tf_op jit(solution)/shard_map/pallas_call | solution.py:615
  83.9 1.1 %shard_map.85 = (bf16[64,512]{1,0:T(8,128)(2,1)}, f32[512,512]{1,0:T(8,128)}, f32[64,512]{1,0:T(8,128)}, f32[64,512]{1,0:T(8,128)}) custom-call(bf16[64,512]{1,0:T(8,128)(2,1)S(1)} %get-tuple-element.12.w1, f32[512,512]{1,0:T(8,128)S(1)} %get-tuple-element.13.h1, f32[64,512]{1,0:T(8,128)S(1)} %get-tuple-element.14.w2t, f32[64,512]{1,0:T(8,128)S(1)} %get-tuple-element.15.h2), custom_call_target="tpu_custom_call" | custom-call | tf_op jit(solution)/shard_map/pallas_call | solution.py:630

commit v7 on v6

--- a/solution.py
+++ b/solution.py
@@ -13,7 +13,7 @@
 ORDER = (1, 3, 2)
 
 SIZES = dict(
-    z=1, a2=12, a3=36, f=8, m=3, nd=4, n=8, hb=4, hf=4, hs=6, h2=3, e1=8, pd=4, pds=4, p=8, ps=4, q=6, qs=6, l=1, ls=1,
+    z=1, a2=12, a3=36, f=8, m=3, nd=4, n=8, hb=4, hf=4, hs=6, h2=3, e1=8, pd=4, pds=4, p=8, ps=4, q=12, qs=6, l=1, ls=1,
     s0=1, s1=3, s2=3, s3=1, s4=3, s5=3, s6=1,
 )
 PLACE, S_ALL = {}, 0
@@ -236,6 +236,19 @@
         return copy(src, src, "hf", 2 * b + p, to_g(3 if p else 1))
 
     far_most = most_of(num[at_g(2)], 0)
+    def code_num(b, d, p, more, most):
+        at = rows(b, p)
+        value = num[at_g(d), at]
+        if more is not None:
+            value += decoded(nqr[1, at], more)
+        nq[d - 1, at] = coded(value, most)
+
+    def start_diag(b):
+        for p in range(2):
+            code_num(b, 2, p, None, far_most)
+            send_diag(b, p).start()
+
+    start_diag(0)
     for d in (2, 1, 3):
         most = far_most if d == 2 else most_of(num[at_g(d)], 0)
         nm[d - 1, :, 0:512] = cs[...]
@@ -243,23 +256,11 @@
         nm[d - 1, :, 640:768] = jnp.broadcast_to(far_most, (8, 128))
         send_marks(d).start()
 
-    def code_num(b, d, p, more, most):
-        at = rows(b, p)
-        value = num[at_g(d), at]
-        if more is not None:
-            value += decoded(nqr[1, at], more)
-        nq[d - 1, at] = coded(value, most)
-
     def mark(d):
         return nm[d - 1, 0:1, 512:640]
 
     def sent_mark(d, k=0):
         return nmr[d - 1, 0:1, 512 + 128 * k : 640 + 128 * k]
-
-    def start_diag(b):
-        for p in range(2):
-            code_num(b, 2, p, None, far_most)
-            send_diag(b, p).start()
 
     def start_own(b):
         for d, p in ((1, 1), (3, 0)):
@@ -272,7 +273,6 @@
             code_num(b, d, p, sent_mark(d, 1), mark(d) + sent_mark(d, 1))
             send_num(b, d, p).start()
 
-    start_diag(0)
     start_own(0)
     start_diag(1)
     read_w2.wait()
@@ -492,13 +492,24 @@
 
     lax.fori_loop(0, 5, second_step, 0)
 
-    def across(h, d):
-        to = to_y(d) if h == 0 else to_x(d)
+    def across(h, d, s):
+        k = 6 * h + 2 * (d - 1) + s
+        return copy(aq.at[h, d - 1, s], aqr.at[h, d - 1, s], "q", k, to(1 - h, d))
+
+    def across_steps(h, d):
         k = 3 * h + d - 1
-        return (
-            copy(aq.at[h, d - 1], aqr.at[h, d - 1], "q", k, to),
-            copy(aps.at[h, d - 1], apr.at[h, d - 1], "qs", k, to),
-        )
+        return copy(aps.at[h, d - 1], apr.at[h, d - 1], "qs", k, to(1 - h, d))
+
+    def add_across(h, s):
+        whole = acc[h, my if h == 0 else mx, mz if s else oz].reshape(4, 8, 512)
+        for d in ORDER:
+            across(h, d, s).wait_recv()
+            if s == 0:
+                across_steps(h, d).wait_recv()
+            q = aqr[h, d - 1, s].astype(jnp.int32).astype(F32).reshape(4, 8, 512)
+            most = apr[h, d - 1, 4 * s : 4 * s + 4].reshape(4, 1, 512)
+            whole += q * (most * (1.0 / TOP))
+        fin[s, h] = whole.reshape(32, 512)
 
     for h in range(2):
         for i in (1, 2):
@@ -516,11 +527,19 @@
             more = decoded(pqr[h, i].reshape(8, 32, 512), psr[h, i].reshape(8, 1, 512))
             acc[h] += more.reshape(4, 2, 32, 512)
             if i == 2:
+                for s in range(2):
+                    for d in ORDER:
+                        v = acc[h, at_y(d) if h == 0 else at_x(d), mz if s else oz].reshape(4, 8, 512)
+                        most = most_of(v, 1)
+                        whole = jnp.round(v * (TOP / most)).astype(jnp.int32)
+                        aq[h, d - 1, s] = whole.reshape(32, 512).astype(I16)
+                        aps[h, d - 1, 4 * s : 4 * s + 4] = most.reshape(4, 512)
+                        if s == 0:
+                            across(h, d, 0).start()
                 for d in ORDER:
-                    v = acc[h, at_y(d) if h == 0 else at_x(d)]
-                    aq[h, d - 1], aps[h, d - 1] = coded_by_8(v)
-                    for go in across(h, d):
-                        go.start()
+                    across_steps(h, d).start()
+                for d in ORDER:
+                    across(h, d, 1).start()
     for d in ORDER:
         all_x(d).wait_recv()
     all_c.start()
@@ -530,16 +549,13 @@
         h2_out[:, 128 * j : 128 * j + 128] = h2b[j]
     rowsum = jnp.concatenate([sg[mc, mx, k : k + 1, 640:768] for k in range(4)], axis=1)
     for h in range(2):
-        whole = acc[h, my if h == 0 else mx]
-        for d in ORDER:
-            for go in across(h, d):
-                go.wait_recv()
-            whole += decoded_by_8(aqr[h, d - 1], apr[h, d - 1])
-        fin[:, h] = whole
-    lq[...], lps[...] = coded_by_8(fin[oz])
+        add_across(h, 0)
+    lq[...], lps[...] = coded_by_8(fin[0])
     last = (copy(lq, lqr, "l", 0, z_pair), copy(lps, lpr, "ls", 0, z_pair))
     for go in last:
         go.start()
+    for h in range(2):
+        add_across(h, 1)
     all_c.wait_recv()
     for j in range(NG):
         for c in range(NC):
@@ -547,7 +563,7 @@
             w2t_out[at, :] = w2tv[at, :] * sg[c, j, :, 0:512] / sg[c, j, :, 512:513]
     for go in last:
         go.wait_recv()
-    w1_num = (fin[mz] + decoded_by_8(lqr[...], lpr[...])).reshape(64, 512)
+    w1_num = (fin[1] + decoded_by_8(lqr[...], lpr[...])).reshape(64, 512)
     w1_now = wg[mx, my, mz, mc].astype(F32).reshape(64, 512)
     w1_out[...] = (w1_now * w1_num / rowsum).astype(BF16)
 
@@ -560,7 +576,7 @@
             for e in ORDER:
                 far(0, h, e, d).wait_send()
                 far(1, h, e, d).wait_send()
-            for sent in across(h, d):
+            for sent in (across(h, d, 0), across(h, d, 1), across_steps(h, d)):
                 sent.wait_send()
         for sent in (send_marks, send_h2, sum_g, sum_x, sum_y, all_x):
             sent(d).wait_send()

time: 85.4 us -> 84.6 us (level)
  Pallas kernels: 84.4 us -> 83.1 us
    pallas_call x1, Pallas kernels: 83.3 us -> 82 us  [on_device(): pl.pallas_call(kernel, out_shape=tuple((pltpu.VMEM(o.shape, o.dtype) for...]
where the time goes in v7:
time: 84.6 us; the launch traced here: 83.8 us
  Pallas kernels  83.1 us (98%)
    pallas_call x1, Pallas kernels, on_device(): pl.pallas_call(kernel, out_shape=tuple((pltpu.VMEM(o.shape, o.dtype) for...  82 us

profile of v7, /device:TPU:1, one launch (start us, length us, event | category | flops | bytes accessed | tf_op | source)
XLA Modules:
  0.0 83.8 jit_solution(16335516727387271166)
XLA Ops:
  0.6 82.0 %shard_map.84 = (bf16[64,512]{1,0:T(8,128)(2,1)S(1)}, f32[512,512]{1,0:T(8,128)S(1)}, f32[64,512]{1,0:T(8,128)S(1)}, f32[64,512]{1,0:T(8,128)S(1)}) custom-call(s32[4,4,2,2,2,32,512]{6,5,4,3,2,1,0:T(8,128)} %bitcast.4, bf16[2,32,512]{2,1,0:T(8,128)(2,1)} %bitcast.6, f32[512,512]{1,0:T(8,128)} %h1.1, f32[64,512]{1,0:T(8,128)} %bitcast.5, f32[64,512]{1,0:T(8,128)} %h2.1), custom_call_target="tpu_custom_call" | custom-call | tf_op jit(solution)/shard_map/pallas_call | solution.py:631
  82.7 1.1 %shard_map.85 = (bf16[64,512]{1,0:T(8,128)(2,1)}, f32[512,512]{1,0:T(8,128)}, f32[64,512]{1,0:T(8,128)}, f32[64,512]{1,0:T(8,128)}) custom-call(bf16[64,512]{1,0:T(8,128)(2,1)S(1)} %get-tuple-element.12.w1, f32[512,512]{1,0:T(8,128)S(1)} %get-tuple-element.13.h1, f32[64,512]{1,0:T(8,128)S(1)} %get-tuple-element.14.w2t, f32[64,512]{1,0:T(8,128)S(1)} %get-tuple-element.15.h2), custom_call_target="tpu_custom_call" | custom-call | tf_op jit(solution)/shard_map/pallas_call | solution.py:646
